TPU v7x, 768 devices: a whole 4x8x12 slice. The times are simulated.
768 devices in a mesh: lat: 96 (over y, z), lon: 8 (over x, core).
Axes of the slice: x: 4, y: 8, z: 12, core: 2. Of those that a mesh axis runs over, the one named last changes fastest.
Arguments:
- grid_in: float32 [196608, 512], P(('lat', 'lon')), may hold values from -6 to 6
- target: float32 [196608, 128], P(('lat', 'lon')), may hold values from -6 to 6
- w_enc: float32 [512, 512], replicated, may hold values from -0.25 to 0.25
- w_mix_self: float32 [2, 512, 512], replicated, may hold values from -0.25 to 0.25
- w_mix_nbr: float32 [2, 512, 512], replicated, may hold values from -0.25 to 0.25
- w_dec: float32 [512, 512], replicated, may hold values from -0.25 to 0.25
- w_out: float32 [512, 128], replicated, may hold values from -0.25 to 0.25
- var_weight: int32 [128], replicated, may hold values from 1 to 8
- g2m_idx: int32 [24576, 8], P(('lat', 'lon')), may hold values from 0 to 12287, as said below
- g2m_w: float32 [24576, 8], P(('lat', 'lon')), may hold values from 0.1 to 1
- mesh_nbr: int32 [24576, 6], P(('lat', 'lon')), may hold values from 0 to 24575, as said below
- m2g_idx: int32 [196608, 4], P(('lat', 'lon')), may hold values from 0 to 24575, as said below
- m2g_w: float32 [196608, 4], P(('lat', 'lon')), may hold values from 0.1 to 1
Outputs:
- pred: float32 [196608, 128], P(('lat', 'lon'))
- loss: float32 [], replicated
- grad_out: float32 [512, 128], replicated
Inputs may be any that keep to these rules, and one draw needn't show every extreme that they name: `g2m_idx`: an entry of row r names a block held by a device whose lat index differs by at most one from that of the device holding row r, and whose lon index differs by at most one, counted cyclically over the 8 tiles; blocks of device d are rows d * 16 onward. `mesh_nbr`: an entry of row r names a mesh node held by a device whose lat index differs by at most one from that of the device holding row r, and whose lon index differs by at most one, counted cyclically over the 8 tiles. `m2g_idx`: an entry of row r names a mesh node held by a device whose lat index differs by at most one from that of the device holding row r, and whose lon index differs by at most one, counted cyclically over the 8 tiles.
All inputs are finite; a program needn't handle non-finite values.
Results may differ from a plain program's by a relative error of at most 0.00028.
Values sent between devices are 32-bit elements; how exact they have to be, the bound alone decides.
A program may use at most 32 MiB of HBM per device.

v0:
```python
import jax
import jax.numpy as jnp
from jax import lax
from jax.sharding import PartitionSpec as P

BS = 16
L = 2


def padded(block, sides, width, periodic):
    for axis, dim in sides:
        count = lax.axis_size(axis)
        forward = [(i, i + 1) for i in range(count - 1)]
        if periodic:
            forward.append((count - 1, 0))
        backward = [(target, source) for source, target in forward]
        low = lax.ppermute(
            lax.slice_in_dim(block, block.shape[dim] - width, None, axis=dim), axis, forward
        )
        high = lax.ppermute(lax.slice_in_dim(block, 0, width, axis=dim), axis, backward)
        block = jnp.concatenate([low, block, high], axis=dim)
    return block


def silu(value):
    return value / (1.0 + jnp.exp(-value))


def matmul(left, right):
    return jnp.dot(left, right, precision=lax.Precision.HIGHEST, preferred_element_type=jnp.float32)


def band_window(table):
    shard_rows = table.shape[0]
    width = table.shape[1]
    n_tiles = lax.axis_size("lon")
    band = lax.axis_index("lat")
    tile = lax.axis_index("lon")
    stacked = table.reshape(1, 1, shard_rows, width)
    three_tiles = padded(stacked, (("lon", 1),), 1, True)
    square = padded(three_tiles, (("lat", 0),), 1, False)
    window = square.reshape(9 * shard_rows, width)

    def locate(index):
        owner = index // shard_rows
        within = index % shard_rows
        src_band = owner // n_tiles
        src_tile = owner % n_tiles
        band_slot = src_band - band + 1
        tile_slot = (src_tile - tile + 1 + n_tiles) % n_tiles
        return (band_slot * 3 + tile_slot) * shard_rows + within

    return (window, locate)


def interp(table, index, weights):
    window, locate = band_window(table)
    local = locate(index)
    rows = jnp.take(window, local.reshape(-1), axis=0).reshape(
        index.shape[0], index.shape[1], table.shape[1]
    )
    total = jnp.einsum("rk,rkd->rd", weights, rows, precision=lax.Precision.HIGHEST)
    return total / jnp.sum(weights, axis=1, keepdims=True)


def mixing(mesh, mesh_nbr, self_weight, nbr_weight):
    window, locate = band_window(mesh)
    local = locate(mesh_nbr)
    rows = jnp.take(window, local.reshape(-1), axis=0).reshape(
        mesh_nbr.shape[0], mesh_nbr.shape[1], mesh.shape[1]
    )
    agg = jnp.sum(rows, axis=1) / mesh_nbr.shape[1]
    center = mesh - jnp.mean(mesh, axis=1, keepdims=True)
    nrm = center / jnp.sqrt(jnp.mean(center * center, axis=1, keepdims=True) + 1e-05)
    return mesh + silu(matmul(nrm, self_weight) + matmul(agg, nbr_weight))


def shards(
    grid_in,
    target,
    w_enc,
    w_mix_self,
    w_mix_nbr,
    w_dec,
    w_out,
    var_weight,
    g2m_idx,
    g2m_w,
    mesh_nbr,
    m2g_idx,
    m2g_w,
):
    width = grid_in.shape[1]
    h_one = grid_in + silu(matmul(grid_in, w_enc))
    blocks = jnp.mean(h_one.reshape(-1, BS, width), axis=1)
    mesh = interp(blocks, g2m_idx, g2m_w)
    for layer in range(L):
        mesh = mixing(mesh, mesh_nbr, w_mix_self[layer], w_mix_nbr[layer])
    back = interp(mesh, m2g_idx, m2g_w)
    hidden = silu(matmul(h_one + back, w_dec))
    pred = matmul(hidden, w_out)
    resid = pred - target
    power_part = jnp.sum(target * target, axis=0)
    err_part = jnp.sum(resid * resid, axis=0)
    weights = var_weight.astype(jnp.float32)
    wsum = jnp.sum(weights)
    grid_total = grid_in.shape[0] * lax.axis_size("lat") * lax.axis_size("lon")
    power = lax.psum(power_part, ("lat", "lon"))
    scale = power / grid_total + 1e-06
    coef = 2.0 * weights / (scale * grid_total * wsum)
    grad_part = matmul(hidden.T, resid * coef[None, :])
    err, grad_out = lax.psum((err_part, grad_part), ("lat", "lon"))
    loss = jnp.sum(weights * err / (scale * grid_total * wsum))
    return (pred, loss, grad_out)


def solution(mesh):
    placed = (
        P(("lat", "lon"), None),
        P(("lat", "lon"), None),
        P(),
        P(),
        P(),
        P(),
        P(),
        P(),
        P(("lat", "lon"), None),
        P(("lat", "lon"), None),
        P(("lat", "lon"), None),
        P(("lat", "lon"), None),
        P(("lat", "lon"), None),
    )
    return jax.shard_map(
        shards,
        mesh=mesh,
        in_specs=placed,
        out_specs=(P(("lat", "lon"), None), P(), P()),
        check_vma=False,
    )
```

profile of v0, /device:TPU:1, one launch (start us, length us, event | category | flops | bytes accessed | tf_op | source)
XLA Modules:
  0.0 697.5 jit_solution(13668405320681656902)
XLA Ops:
  7.3 1.1 copy-done
  8.4 3.3 bitcast_reduce_fusion
  11.7 2.6 collective-permute-start
  14.3 7.9 %collective-permute-start.1 = (f32[1,1,16,512]{3,2,1,0:T(8,128)S(1)}, f32[1,1,16,512]{3,2,1,0:T(8,128)S(1)}, u32[]{:S(2)}, u32[]{:S(2)}) collective-permute-start(f32[1,1,16,512]{3,2,1,0:T(8,128)S(1)} %multiply_bitcast_fusion), channel_id=1, source_target_pairs={{1,0},{2,1},{3,2},{4,3},{5,4},{6,5},{7,6},{0,7},{9,8},{10,9},{11,1... | collective-permute-start | bytes 98312 | tf_op jit(solution)/shard_map/ppermute | solution.py:20
  22.2 0.1 copy.21
  22.3 0.1 reshape.173
  22.6 0.1 reshape.170
  22.7 0.1 copy.22
  22.9 0.1 reshape.180
  23.0 0.1 copy.19
  23.2 0.8 copy.18
  24.0 0.6 reduce_sum.125
  24.6 0.1 copy.25
  24.7 1.3 collective-permute-start.2
  26.0 1.3 collective-permute-start.3
  27.4 0.3 collective-permute-done.2
  27.7 3.7 collective-permute-done.3
  31.4 1.0 gather_fusion
  32.4 0.7 fusion.17
  33.1 0.2 fusion.86
  33.3 0.2 fusion.85
  33.5 4.1 collective-permute-start.5
  37.6 0.7 collective-permute-done.4
  38.3 0.2 collective-permute-done.5
  38.5 1.7 collective-permute-start.6
  40.2 1.3 collective-permute-start.7
  41.5 2.0 fusion.6
  43.5 5.2 collective-permute-done.7
  48.7 1.6 gather_fusion.2
  50.3 2.0 broadcast_select_fusion.1
  52.3 1.8 reshape.174
  54.2 1.2 reduce_sum.121
  55.4 0.8 fusion.89
  56.2 2.7 collective-permute-start.8
  59.0 0.2 collective-permute-start.9
  59.2 0.2 multiply_reduce_fusion.2
  59.4 0.9 collective-permute-done.8
  60.3 2.7 collective-permute-done.9
  63.0 4.6 collective-permute-start.10
  67.6 1.3 collective-permute-start.11
  68.9 2.0 fusion.3
  70.8 4.6 collective-permute-done.11
  75.5 1.6 gather_fusion.3
  77.1 2.0 broadcast_select_fusion
  79.1 1.8 reshape.177
  81.0 1.2 reduce_sum.124
  82.2 0.7 add_bitcast_fusion
  82.9 1.9 collective-permute-start.12
  84.8 0.6 convert_reduce_fusion
  86.1 2.7 collective-permute-done.13
  88.8 4.7 collective-permute-start.14
  93.5 1.5 collective-permute-start.15
  95.0 1.9 collective-permute-done.14
  96.9 3.8 collective-permute-done.15
  100.7 4.9 gather_fusion.1
  105.6 1.9 gather.18
  107.6 4.3 fusion
  111.9 1.3 add_divide_fusion
  113.2 0.6 multiply_reduce_fusion
  113.9 113.5 %all-reduce = (f32[128]{0:T(128)S(1)}, f32[128]{0:T(128)S(1)}) all-reduce(f32[128]{0:T(128)S(1)} %get-tuple-element.5, f32[128]{0:T(128)S(1)} %get-tuple-element.4), channel_id=1, replica_groups=mesh['lat'=96,'lon'=8] {'lat','lon'}, use_global_device_ids=true, to_apply=%region_10.12 | all-reduce | flops 256 | bytes 2048 | tf_op jit(solution)/shard_map/psum | solution.py:112
  227.4 0.6 multiply_divide_fusion
  228.0 1.7 fusion.24
  229.7 459.2 %all-reduce.3.cloned.1.call-done = f32[512,128]{1,0:T(8,128)} async-done(((f32[512,128]{1,0:T(8,128)}), f32[512,128]{1,0:T(8,128)}) %all-reduce.3.cloned.1.call-update) | async-done | bytes 262160 | tf_op jit(solution)/shard_map/psum | solution.py:112
  688.9 1.7 copy.46
  (68 shorter events, 0.8 us)
Async XLA Ops:
  7.2 1.2 copy-start
  7.2 15.0 %copy-start.9 = (s32[32,6]{0,1:T(8,128)S(1)}, s32[32,6]{0,1:T(8,128)}, u32[]{:S(2)}) copy-start(s32[32,6]{0,1:T(8,128)} %param.25) | copy-start | bytes 2308
  7.2 15.3 %copy-start.10 = (s32[32,8]{0,1:T(8,128)S(1)}, s32[32,8]{0,1:T(8,128)}, u32[]{:S(2)}) copy-start(s32[32,8]{0,1:T(8,128)} %param.23) | copy-start | bytes 3076
  7.2 15.5 %copy-start.11 = (s32[256,4]{0,1:T(4,128)S(1)}, s32[256,4]{0,1:T(4,128)}, u32[]{:S(2)}) copy-start(s32[256,4]{0,1:T(4,128)} %param.26) | copy-start | bytes 12292
  7.2 15.9 %copy-start.7 = (f32[32,8]{0,1:T(8,128)S(1)}, f32[32,8]{0,1:T(8,128)}, u32[]{:S(2)}) copy-start(f32[32,8]{0,1:T(8,128)} %param.24) | copy-start | bytes 3076
  7.2 16.8 %copy-start.8 = (f32[256,4]{0,1:T(4,128)S(1)}, f32[256,4]{0,1:T(4,128)}, u32[]{:S(2)}) copy-start(f32[256,4]{0,1:T(4,128)} %param.27) | copy-start | bytes 12292
  7.2 681.7 %all-reduce.3.cloned.1.call-start = ((), (), s32[]{:S(2)}) async-start(), calls=%async_computation | async-start | bytes 524288 | tf_op jit(solution)/shard_map/psum | solution.py:112
  11.7 13.1 %collective-permute-start = (f32[1,1,16,512]{3,2,1,0:T(8,128)S(1)}, f32[1,1,16,512]{3,2,1,0:T(8,128)S(1)}, u32[]{:S(2)}, u32[]{:S(2)}) collective-permute-start(f32[1,1,16,512]{3,2,1,0:T(8,128)S(1)} %multiply_bitcast_fusion), channel_id=1, source_target_pairs={{0,1},{1,2},{2,3},{3,4},{4,5},{5,6},{6,7},{7,0},{8,9},{9,10},{10,1... | collective-permute-start | bytes 98312 | tf_op jit(solution)/shard_map/ppermute | solution.py:17
  14.3 10.5 %collective-permute-start.1 = (f32[1,1,16,512]{3,2,1,0:T(8,128)S(1)}, f32[1,1,16,512]{3,2,1,0:T(8,128)S(1)}, u32[]{:S(2)}, u32[]{:S(2)}) collective-permute-start(f32[1,1,16,512]{3,2,1,0:T(8,128)S(1)} %multiply_bitcast_fusion), channel_id=1, source_target_pairs={{1,0},{2,1},{3,2},{4,3},{5,4},{6,5},{7,6},{0,7},{9,8},{10,9},{11,1... | collective-permute-start | bytes 98312 | tf_op jit(solution)/shard_map/ppermute | solution.py:20
  24.7 2.9 collective-permute-start.2
  26.0 5.4 collective-permute-start.3
  33.5 4.9 collective-permute-start.4
  33.5 5.0 collective-permute-start.5
  38.5 5.0 collective-permute-start.6
  40.2 8.4 %collective-permute-start.7 = (f32[1,3,32,512]{3,2,1,0:T(8,128)S(1)}, f32[1,3,32,512]{3,2,1,0:T(8,128)S(1)}, u32[]{:S(2)}, u32[]{:S(2)}) collective-permute-start(f32[1,3,32,512]{3,2,1,0:T(8,128)S(1)} %pad_maximum_fusion.4), channel_id=1, source_target_pairs={{8,0},{16,8},{24,16},{32,24},{40,32},{48,40},{56,48},{64,56},{72,6... | collective-permute-start | bytes 589832 | tf_op jit(solution)/shard_map/ppermute | solution.py:20
  50.3 5.0 copy-start.1
  56.2 4.1 collective-permute-start.8
  59.0 4.0 collective-permute-start.9
  63.0 7.9 %collective-permute-start.10 = (f32[1,3,32,512]{3,2,1,0:T(8,128)S(1)}, f32[1,3,32,512]{3,2,1,0:T(8,128)S(1)}, u32[]{:S(2)}, u32[]{:S(2)}) collective-permute-start(f32[1,3,32,512]{3,2,1,0:T(8,128)S(1)} %pad_maximum_fusion.5), channel_id=1, source_target_pairs={{0,8},{8,16},{16,24},{24,32},{32,40},{40,48},{48,56},{56,64},{64,7... | collective-permute-start | bytes 589832 | tf_op jit(solution)/shard_map/ppermute | solution.py:17
  67.6 7.9 %collective-permute-start.11 = (f32[1,3,32,512]{3,2,1,0:T(8,128)S(1)}, f32[1,3,32,512]{3,2,1,0:T(8,128)S(1)}, u32[]{:S(2)}, u32[]{:S(2)}) collective-permute-start(f32[1,3,32,512]{3,2,1,0:T(8,128)S(1)} %pad_maximum_fusion.5), channel_id=1, source_target_pairs={{8,0},{16,8},{24,16},{32,24},{40,32},{48,40},{56,48},{64,56},{72,6... | collective-permute-start | bytes 589832 | tf_op jit(solution)/shard_map/ppermute | solution.py:20
  77.1 5.0 copy-start.2
  77.1 7.7 %copy-start.13 = (s32[128]{0:T(128)S(1)}, s32[128]{0:T(128)}, u32[]{:S(2)}) copy-start(s32[128]{0:T(128)} %param.22) | copy-start | bytes 1540
  82.9 3.2 collective-permute-start.12
  84.8 4.0 collective-permute-start.13
  88.8 8.1 %collective-permute-start.14 = (f32[1,3,32,512]{3,2,1,0:T(8,128)S(1)}, f32[1,3,32,512]{3,2,1,0:T(8,128)S(1)}, u32[]{:S(2)}, u32[]{:S(2)}) collective-permute-start(f32[1,3,32,512]{3,2,1,0:T(8,128)S(1)} %pad_maximum_fusion.6), channel_id=1, source_target_pairs={{0,8},{8,16},{16,24},{24,32},{32,40},{40,48},{48,56},{56,64},{64,7... | collective-permute-start | bytes 589832 | tf_op jit(solution)/shard_map/ppermute | solution.py:17
  93.5 7.2 %collective-permute-start.15 = (f32[1,3,32,512]{3,2,1,0:T(8,128)S(1)}, f32[1,3,32,512]{3,2,1,0:T(8,128)S(1)}, u32[]{:S(2)}, u32[]{:S(2)}) collective-permute-start(f32[1,3,32,512]{3,2,1,0:T(8,128)S(1)} %pad_maximum_fusion.6), channel_id=1, source_target_pairs={{8,0},{16,8},{24,16},{32,24},{40,32},{48,40},{56,48},{64,56},{72,6... | collective-permute-start | bytes 589832 | tf_op jit(solution)/shard_map/ppermute | solution.py:20
  105.6 1.9 copy-start.6
  107.5 4.3 copy-start.12
  107.5 4.3 copy-start.14
  107.5 4.3 copy-start.15
  107.5 4.3 copy-start.16
  111.9 1.3 copy-start.3
  111.9 1.3 copy-start.5
  113.8 576.8 %copy-start.4 = (f32[256,128]{1,0:T(8,128)}, f32[256,128]{1,0:T(8,128)S(1)}, u32[]{:S(2)}) copy-start(f32[256,128]{1,0:T(8,128)S(1)} %get-tuple-element.21) | copy-start | bytes 393220
Sparse Core Ops, SparseCore 0:
  229.8 459.0 all-reduce.2
where the time goes:
time: 698 us; the launch traced here: 697 us
  waiting for transfers between devices  486 us (70%)
  blocking collectives  114 us (16%)
  starting transfers between devices  37.2 us (5%)
  local copies, waits for them, and re-layouts  19.2 us (3%)
  matrix products  17.3 us (2%)
  between operations  15.2 us (2%)
  other arithmetic  9.14 us (1%)
    psum x1, waiting for transfers between devices, shards(): err, grad_out = lax.psum((err_part, grad_part), ('lat', 'lon'))  459 us
    psum x1, blocking collectives, shards(): err, grad_out = lax.psum((err_part, grad_part), ('lat', 'lon'))  114 us
    ppermute x8, waiting for transfers between devices, padded(): lax.ppermute(lax.slice_in_dim(block, 0, width, axis=dim), axis, backward)  22.9 us
    ppermute x8, starting transfers between devices, padded(): lax.ppermute(lax.slice_in_dim(block, block.shape[dim] - width, None, axis...  19.6 us
    ppermute x8, starting transfers between devices, padded(): lax.ppermute(lax.slice_in_dim(block, 0, width, axis=dim), axis, backward)  17.6 us
  transfers between devices with their start and end apart: 17, of which 13 were waited for; matrix products, arithmetic and copies ran while one was open for 1% of the time, Pallas kernels for 0%

commit v1 on v0

v1 whole, which is shorter than its diff:
```python
import functools

import jax
import jax.numpy as jnp
from jax import lax
from jax.experimental import pallas as pl
from jax.experimental.pallas import tpu as pltpu
from jax.sharding import PartitionSpec as P

BS = 16
L = 2
NZ = 12
EPS = 1e-05
F32 = jnp.float32
BF16 = jnp.bfloat16
MESH = pl.DeviceIdType.MESH


def split(value):
    high = value.astype(BF16)
    low = (value - high.astype(F32)).astype(BF16)
    return high, low


def dot(left, right):
    return jnp.dot(left, right, preferred_element_type=F32)


def mm3(left, right):
    (lh, ll), (rh, rl) = left, right
    return dot(lh, rh) + (dot(lh, rl) + dot(ll, rh))


def silu(value):
    return value / (1.0 + jnp.exp(-value))


def span(index, size):
    return pl.ds(pl.multiple_of(index * size, size), size)


def farthest_first(count):
    return sorted(range(count), key=lambda d: (-min(d, count - d), d))


def program_kernel(
    n_lat,
    n_lon,
    nz,
    grid_hbm,
    target_hbm,
    w_enc_hbm,
    w_self_hbm,
    w_nbr_hbm,
    w_dec_hbm,
    w_out_hbm,
    var_weight,
    g_idx_hbm,
    g_w_hbm,
    nbr_hbm,
    m_idx_hbm,
    m_w_hbm,
    pred_hbm,
    loss_ref,
    grad_hbm,
    grid,
    target,
    w_f32,
    w_out,
    g_idx,
    g_w,
    nbr,
    m_idx,
    m_w,
    w_bf,
    w_out_bf,
    h_bf,
    h_dec,
    back_bf,
    win0,
    win1,
    win2,
    win3,
    pred,
    grad,
    s1,
    s2_src,
    s2,
    s3,
    total,
    st1,
    st2,
    st3,
    in_sem,
    out_sem,
    halo_recv,
    halo_send,
    s1_recv,
    s4_recv,
    ar_recv,
    ar_send,
):
    lat = lax.axis_index("lat")
    lon = lax.axis_index("lon")
    ny = n_lat // nz
    y = lat // nz
    z = lat % nz
    points, width = grid.shape
    n_var = target.shape[1]
    piece = s3.shape[1]
    lon_rows = ny * piece
    grid_total = float(points * n_lat * n_lon)

    def at_lat(step):
        return ((lat + step + n_lat) % n_lat, lon)

    def at_lon(step):
        return (lat, (lon + step + n_lon) % n_lon)

    def at_y(step):
        return (((y + step) % ny) * nz + z, lon)

    def at_z(step):
        return (y * nz + (z + step) % nz, lon)

    peers = [at_lat(1), at_lat(-1)]
    peers += [at_lon(d) for d in range(1, n_lon)]
    peers += [at_y(d) for d in range(1, ny)]
    peers += [at_z(d) for d in range(1, nz)]

    barrier = pltpu.get_barrier_semaphore()
    for peer in peers:
        pl.semaphore_signal(barrier, inc=1, device_id=peer, device_id_type=MESH)

    def load(source, dest, slot):
        return pltpu.make_async_copy(source, dest, in_sem.at[slot])

    first = [
        load(g_idx_hbm, g_idx, 0),
        load(g_w_hbm, g_w, 1),
        load(grid_hbm, grid, 2),
        load(w_enc_hbm, w_f32.at[0], 3),
    ]
    later = [
        load(nbr_hbm, nbr, 4),
        load(m_idx_hbm, m_idx, 5),
        load(m_w_hbm, m_w, 6),
        load(w_dec_hbm, w_f32.at[1], 7),
        load(w_self_hbm.at[0], w_f32.at[2], 8),
        load(w_nbr_hbm.at[0], w_f32.at[3], 9),
        load(w_self_hbm.at[1], w_f32.at[4], 10),
        load(w_nbr_hbm.at[1], w_f32.at[5], 11),
        load(w_out_hbm, w_out, 12),
        load(target_hbm, target, 13),
    ]
    for copy in first:
        copy.start()

    def split_weight(which):
        def body(step, carry):
            rows = span(step, 64)
            high, low = split(w_f32[which, rows, :])
            w_bf[which, 0, rows, :] = high
            w_bf[which, 1, rows, :] = low
            return carry

        lax.fori_loop(0, width // 64, body, 0)

    def weight(which):
        return w_bf[which, 0], w_bf[which, 1]

    def locate(index, rows):
        shift = rows.bit_length() - 1
        lon_shift = n_lon.bit_length() - 1
        owner = index >> shift
        within = index & (rows - 1)
        band_slot = (owner >> lon_shift) - lat + 1
        tile_slot = ((owner & (n_lon - 1)) - lon + 1 + n_lon) & (n_lon - 1)
        return ((band_slot * 3 + tile_slot) << shift) + within

    def select(local, factors, columns):
        place = lax.broadcasted_iota(jnp.int32, (local.shape[0], columns), 1)
        chosen = jnp.zeros((local.shape[0], columns), F32)
        for k in range(local.shape[1]):
            value = 1.0 if factors is None else factors[:, k : k + 1]
            chosen = chosen + jnp.where(place == local[:, k : k + 1], value, 0.0)
        return chosen

    def send(win, rows, turn, source, dest, group, peer):
        pltpu.make_async_remote_copy(
            src_ref=win.at[pl.ds(source * rows, rows)],
            dst_ref=win.at[pl.ds(dest * rows, rows)],
            send_sem=halo_send.at[turn],
            recv_sem=halo_recv.at[turn, group],
            device_id=peer,
            device_id_type=MESH,
        ).start()

    def halo_start(win, rows, turn):
        send(win, rows, turn, 4, 1, 0, at_lat(1))
        send(win, rows, turn, 4, 7, 1, at_lat(-1))
        send(win, rows, turn, 4, 3, 2, at_lon(1))
        send(win, rows, turn, 4, 5, 2, at_lon(-1))

    def halo_wait(win, rows, turn, group, count):
        part = win.at[pl.ds(0, count * rows)]
        pltpu.make_async_copy(part, part, halo_recv.at[turn, group]).wait()

    def halo_forward(win, rows, turn):
        halo_wait(win, rows, turn, 0, 1)
        send(win, rows, turn, 1, 0, 3, at_lon(1))
        send(win, rows, turn, 1, 2, 3, at_lon(-1))
        halo_wait(win, rows, turn, 1, 1)
        send(win, rows, turn, 7, 6, 3, at_lon(1))
        send(win, rows, turn, 7, 8, 3, at_lon(-1))

    def halo_sent(win, rows, turn):
        part = win.at[pl.ds(0, 8 * rows)]
        pltpu.make_async_copy(part, part, halo_send.at[turn]).wait()

    blocks_dev = points // BS
    mesh_dev = nbr.shape[0]
    first[0].wait()
    first[1].wait()
    g_weights = g_w[...]
    g_select = split(select(locate(g_idx[...], blocks_dev), g_weights, 9 * blocks_dev))
    g_total = jnp.sum(g_weights, axis=1, keepdims=True)

    first[3].wait()
    for copy in later:
        copy.start()
    split_weight(0)
    first[2].wait()

    def encode(step, carry):
        rows = span(step, 128)
        value = grid[rows, :]
        h_one = value + silu(mm3(split(value), weight(0)))
        high, low = split(h_one)
        h_bf[0, rows, :] = high
        h_bf[1, rows, :] = low
        means = jnp.sum(h_one.reshape(128 // BS, BS, width), axis=1) * (1.0 / BS)
        start = pl.multiple_of(4 * blocks_dev + step * (128 // BS), 128 // BS)
        win0[pl.ds(start, 128 // BS), :] = means
        return carry

    lax.fori_loop(0, points // 128, encode, 0)
    pl.semaphore_wait(barrier, len(peers))
    halo_start(win0, blocks_dev, 0)

    later[0].wait()
    a_select = select(locate(nbr[...], mesh_dev), None, 9 * mesh_dev).astype(BF16)
    later[4].wait()
    split_weight(2)
    later[5].wait()
    split_weight(3)
    halo_forward(win0, blocks_dev, 0)
    later[3].wait()
    split_weight(1)

    def hidden_part(step, carry):
        rows = span(step, 128)
        h_dec[rows, :] = mm3((h_bf[0, rows, :], h_bf[1, rows, :]), weight(1))
        return carry

    lax.fori_loop(0, points // 128, hidden_part, 0)
    halo_wait(win0, blocks_dev, 0, 2, 2)
    halo_wait(win0, blocks_dev, 0, 3, 4)

    mesh = mm3(g_select, split(win0[...])) / g_total
    wins = (win1, win2, win3)

    def own(win):
        return pl.ds(4 * mesh_dev, mesh_dev)

    for layer in range(L):
        win = wins[layer]
        win[own(win), :] = mesh
        halo_start(win, mesh_dev, layer + 1)
        center = mesh - jnp.mean(mesh, axis=1, keepdims=True)
        spread = jnp.mean(center * center, axis=1, keepdims=True)
        nrm = center / jnp.sqrt(spread + EPS)
        self_part = mm3(split(nrm), weight(2 + 2 * layer))
        halo_forward(win, mesh_dev, layer + 1)
        if layer == 0:
            for slot, which in ((6, 4), (7, 5)):
                later[slot].wait()
                split_weight(which)
        else:
            later[1].wait()
            later[2].wait()

            def build(step, carry):
                rows = span(step, 64)
                factors = m_w[rows, :]
                factors = factors / jnp.sum(factors, axis=1, keepdims=True)
                chosen = select(locate(m_idx[rows, :], mesh_dev), factors, 9 * mesh_dev)
                high, low = split(chosen)
                back_bf[0, rows, :] = high
                back_bf[1, rows, :] = low
                return carry

            lax.fori_loop(0, points // 64, build, 0)
        halo_wait(win, mesh_dev, layer + 1, 2, 2)
        halo_wait(win, mesh_dev, layer + 1, 3, 4)
        high, low = split(win[...])
        agg = (dot(a_select, high) + dot(a_select, low)) / float(nbr.shape[1])
        mesh = mesh + silu(self_part + mm3(split(agg), weight(3 + 2 * layer)))

    win3[own(win3), :] = mm3(split(mesh), weight(1))
    halo_start(win3, mesh_dev, 3)
    later[8].wait()
    high, low = split(w_out[...])
    w_out_bf[0] = high
    w_out_bf[1] = low
    halo_forward(win3, mesh_dev, 3)
    later[9].wait()
    power = jnp.sum(target[...] * target[...], axis=0, keepdims=True)
    weights = var_weight[...].astype(F32)
    wsum = jnp.sum(weights, axis=1, keepdims=True)
    halo_wait(win3, mesh_dev, 3, 2, 2)
    halo_wait(win3, mesh_dev, 3, 3, 4)

    table = split(win3[...])
    w_out_parts = (w_out_bf[0], w_out_bf[1])
    err = jnp.zeros((1, n_var), F32)
    for step in range(points // 128):
        rows = pl.ds(step * 128, 128)
        hidden = silu(h_dec[rows, :] + mm3((back_bf[0, rows, :], back_bf[1, rows, :]), table))
        hh, hl = split(hidden)
        out = mm3((hh, hl), w_out_parts)
        pred[rows, :] = out
        resid = out - target[rows, :]
        err = err + jnp.sum(resid * resid, axis=0, keepdims=True)
        part = mm3((hh.T, hl.T), split(resid))
        if step == 0:
            grad[...] = part
        else:
            grad[...] += part
    pred_copy = pltpu.make_async_copy(pred, pred_hbm, out_sem.at[0])
    pred_copy.start()

    def push(source, dest, stage, recv, peer):
        pltpu.make_async_remote_copy(
            src_ref=source,
            dst_ref=dest,
            send_sem=ar_send.at[stage],
            recv_sem=recv,
            device_id=peer,
            device_id_type=MESH,
        ).start()

    def drain(part, sem):
        pltpu.make_async_copy(part, part, sem).wait()

    y_order = farthest_first(ny)
    lon_order = [d for d in farthest_first(n_lon) if d]
    z_order = [d for d in farthest_first(nz) if d]

    st1[lon] = jnp.concatenate([power, err], axis=0)
    for d in lon_order:
        push(st1.at[lon], st1.at[lon], 0, ar_recv.at[0], at_lon(d))
    for off in y_order:
        j = (y + off) % ny
        for d in lon_order:
            block = ((lon + d) % n_lon) * ny + j
            push(grad.at[span(block, piece)], s1.at[j, lon], 1, s1_recv.at[j], at_lon(d))

    drain(st1.at[pl.ds(0, n_lon - 1)], ar_recv.at[0])
    stats = st1[0]
    for i in range(1, n_lon):
        stats = stats + st1[i]
    st2[y] = stats
    for d in range(1, ny):
        push(st2.at[y], st2.at[y], 2, ar_recv.at[1], at_y(d))

    kept = None
    for off in y_order:
        j = (y + off) % ny
        drain(s1.at[j, pl.ds(0, n_lon - 1)], s1_recv.at[j])
        value = grad[span(lon * ny + j, piece), :]
        for d in range(1, n_lon):
            value = value + s1[j, (lon + d) % n_lon]
        if off:
            s2_src[j] = value
            push(s2_src.at[j], s2.at[y], 3, ar_recv.at[2], at_y(off))
        else:
            kept = value

    drain(st2.at[pl.ds(0, ny - 1)], ar_recv.at[1])
    stats = st2[0]
    for i in range(1, ny):
        stats = stats + st2[i]
    st3[z] = stats
    for d in z_order:
        push(st3.at[z], st3.at[z], 4, ar_recv.at[3], at_z(d))

    drain(s2.at[pl.ds(0, ny - 1)], ar_recv.at[2])
    for off in range(1, ny):
        kept = kept + s2[(y + off) % ny]
    s3[z] = kept
    for d in z_order:
        push(s3.at[z], s3.at[z], 5, ar_recv.at[4], at_z(d))

    drain(st3.at[pl.ds(0, nz - 1)], ar_recv.at[3])
    stats = st3[0]
    for i in range(1, nz):
        stats = stats + st3[i]
    scale = stats[0:1] / grid_total + 1e-06
    norm = scale * grid_total * wsum
    loss = jnp.sum(weights * stats[1:2] / norm, axis=1, keepdims=True)
    loss_ref[...] = jnp.broadcast_to(loss, loss_ref.shape)
    coef = 2.0 * weights / norm

    drain(s3.at[pl.ds(0, nz - 1)], ar_recv.at[4])
    value = s3[0]
    for i in range(1, nz):
        value = value + s3[i]
    mine = span(lon * ny + y, piece)
    total[mine, :] = value * coef
    for off in y_order:
        if off:
            push(total.at[mine], total.at[mine], 6, s4_recv.at[y], at_y(off))
    for d in lon_order:
        push(total.at[mine], total.at[mine], 7, ar_recv.at[5], at_lon(d))
    for off in reversed(y_order):
        if off:
            j = (y + off) % ny
            block = span(lon * ny + j, piece)
            drain(total.at[block], s4_recv.at[j])
            for d in lon_order:
                push(total.at[block], total.at[block], 7, ar_recv.at[5], at_lon(d))
    drain(total.at[pl.ds(0, (n_lon - 1) * lon_rows)], ar_recv.at[5])
    grad_copy = pltpu.make_async_copy(total, grad_hbm, out_sem.at[1])
    grad_copy.start()

    halo_sent(win0, blocks_dev, 0)
    for turn, win in enumerate(wins):
        halo_sent(win, mesh_dev, turn + 1)
    drain(st1.at[pl.ds(0, n_lon - 1)], ar_send.at[0])
    drain(grad.at[pl.ds(0, (n_lon - 1) * lon_rows)], ar_send.at[1])
    drain(st2.at[pl.ds(0, ny - 1)], ar_send.at[2])
    drain(s2.at[pl.ds(0, ny - 1)], ar_send.at[3])
    drain(st3.at[pl.ds(0, nz - 1)], ar_send.at[4])
    drain(s3.at[pl.ds(0, nz - 1)], ar_send.at[5])
    drain(total.at[pl.ds(0, (ny - 1) * piece)], ar_send.at[6])
    drain(total.at[pl.ds(0, (n_lon - 1) * lon_rows)], ar_send.at[7])
    pred_copy.wait()
    grad_copy.wait()


def shards(
    nz,
    grid_in,
    target,
    w_enc,
    w_mix_self,
    w_mix_nbr,
    w_dec,
    w_out,
    var_weight,
    g2m_idx,
    g2m_w,
    mesh_nbr,
    m2g_idx,
    m2g_w,
):
    n_lat = lax.axis_size("lat")
    n_lon = lax.axis_size("lon")
    ny = n_lat // nz
    points, width = grid_in.shape
    n_var = target.shape[1]
    mesh_dev = mesh_nbr.shape[0]
    blocks_dev = points // BS
    piece = width // (n_lon * ny)
    window = 9 * mesh_dev
    hbm = pl.BlockSpec(memory_space=pl.ANY)
    vmem = pl.BlockSpec(memory_space=pltpu.VMEM)
    pred, loss, grad = pl.pallas_call(
        functools.partial(program_kernel, n_lat, n_lon, nz),
        name="forecast_step",
        out_shape=(
            jax.ShapeDtypeStruct((points, n_var), F32),
            jax.ShapeDtypeStruct((1, n_var), F32),
            jax.ShapeDtypeStruct((width, n_var), F32),
        ),
        in_specs=[hbm] * 7 + [vmem] + [hbm] * 5,
        out_specs=(hbm, vmem, hbm),
        scratch_shapes=[
            pltpu.VMEM((points, width), F32),
            pltpu.VMEM((points, n_var), F32),
            pltpu.VMEM((6, width, width), F32),
            pltpu.VMEM((width, n_var), F32),
            pltpu.VMEM(g2m_idx.shape, jnp.int32),
            pltpu.VMEM(g2m_w.shape, F32),
            pltpu.VMEM(mesh_nbr.shape, jnp.int32),
            pltpu.VMEM(m2g_idx.shape, jnp.int32),
            pltpu.VMEM(m2g_w.shape, F32),
            pltpu.VMEM((6, 2, width, width), BF16),
            pltpu.VMEM((2, width, n_var), BF16),
            pltpu.VMEM((2, points, width), BF16),
            pltpu.VMEM((points, width), F32),
            pltpu.VMEM((2, points, window), BF16),
            pltpu.VMEM((9 * blocks_dev, width), F32),
            pltpu.VMEM((window, width), F32),
            pltpu.VMEM((window, width), F32),
            pltpu.VMEM((window, width), F32),
            pltpu.VMEM((points, n_var), F32),
            pltpu.VMEM((width, n_var), F32),
            pltpu.VMEM((ny, n_lon, piece, n_var), F32),
            pltpu.VMEM((ny, piece, n_var), F32),
            pltpu.VMEM((ny, piece, n_var), F32),
            pltpu.VMEM((nz, piece, n_var), F32),
            pltpu.VMEM((width, n_var), F32),
            pltpu.VMEM((n_lon, 2, n_var), F32),
            pltpu.VMEM((ny, 2, n_var), F32),
            pltpu.VMEM((nz, 2, n_var), F32),
            pltpu.SemaphoreType.DMA((14,)),
            pltpu.SemaphoreType.DMA((2,)),
            pltpu.SemaphoreType.DMA((4, 4)),
            pltpu.SemaphoreType.DMA((4,)),
            pltpu.SemaphoreType.DMA((ny,)),
            pltpu.SemaphoreType.DMA((ny,)),
            pltpu.SemaphoreType.DMA((6,)),
            pltpu.SemaphoreType.DMA((8,)),
        ],
        compiler_params=pltpu.CompilerParams(collective_id=0, has_side_effects=True),
    )(
        grid_in,
        target,
        w_enc,
        w_mix_self,
        w_mix_nbr,
        w_dec,
        w_out,
        var_weight.reshape(1, n_var),
        g2m_idx,
        g2m_w,
        mesh_nbr,
        m2g_idx,
        m2g_w,
    )
    return (pred, loss[0, 0], grad)


def solution(mesh, nz=NZ):
    rows = P(("lat", "lon"), None)
    placed = (rows, rows, P(), P(), P(), P(), P(), P(), rows, rows, rows, rows, rows)
    return jax.shard_map(
        functools.partial(shards, nz),
        mesh=mesh,
        in_specs=placed,
        out_specs=(rows, P(), P()),
        check_vma=False,
    )
```

time: 698 us -> 88.5 us (0.13)
  waiting for transfers between devices: 486 us -> 0 us
  blocking collectives: 114 us -> 0 us
  Pallas kernels: 0 us -> 75.4 us
  starting transfers between devices: 37.2 us -> 0 us
  matrix products: 17.3 us -> 0 us
  between operations: 15.2 us -> 2.45 us
  other arithmetic: 9.14 us -> 0 us
  local copies, waits for them, and re-layouts: 19.2 us -> 10.3 us
    psum x1 -> x0, waiting for transfers between devices: 459 us -> none  [shards(): err, grad_out = lax.psum((err_part, grad_part), ('lat', 'lon'))]
    psum x1 -> x0, blocking collectives: 114 us -> none  [shards(): err, grad_out = lax.psum((err_part, grad_part), ('lat', 'lon'))]
    pallas_call x0 -> x1, Pallas kernels: none -> 75.4 us  [shards(): pl.pallas_call(functools.partial(program_kernel, n_lat, n_lon, nz), name=...]
    ppermute x16 -> x0, starting transfers between devices: 37.1 us -> none  [the longest x8 19.6 us: padded(): lax.ppermute(lax.slice_in_dim(block, block.shape[dim] - width, None, axis...]
    ppermute x16 -> x0, waiting for transfers between devices: 26.7 us -> none  [the longest x8 22.9 us: padded(): lax.ppermute(lax.slice_in_dim(block, 0, width, axis=dim), axis, backward)]
    dot_general x10 -> x0, matrix products: 17.3 us -> none  [the longest x8 12.3 us: matmul(): jnp.dot(left, right, precision=lax.Precision.HIGHEST, preferred_element_t...]
    gather x5 -> x0, local copies, waits for them, and re-layouts: 11 us -> none  [the longest x3 7.73 us: interp(): jnp.take(window, local.reshape(-1), axis=0)]
    unnamed x37 -> x7, local copies, waits for them, and re-layouts: 3.08 us -> 10.3 us
  transfers between devices with their start and end apart: 17 -> 0, of which waited for: 13 -> 0; matrix products, arithmetic and copies ran while one was open for 1% -> 0% of each run, Pallas kernels for 0% -> 0%
where the time goes in v1:
time: 88.5 us; the launch traced here: 88.1 us
  Pallas kernels  75.4 us (85%)
  local copies, waits for them, and re-layouts  10.3 us (12%)
  between operations  2.45 us (3%)
    pallas_call x1, Pallas kernels, shards(): pl.pallas_call(functools.partial(program_kernel, n_lat, n_lon, nz), name=...  75.4 us
    unnamed x7, local copies, waits for them, and re-layouts  10.3 us

profile of v1, /device:TPU:1, one launch (start us, length us, event | category | flops | bytes accessed | tf_op | source)
XLA Modules:
  0.0 88.1 jit_solution(12701728060843739899)
XLA Ops:
  0.6 1.4 %copy.16.g_idx_hbm = s32[32,8]{1,0:T(8,128)} copy(s32[32,8]{0,1:T(8,128)} %param.21) | data formatting | bytes 2048 | tf_op args[8]
  2.0 1.4 %copy.17.g_w_hbm = f32[32,8]{1,0:T(8,128)} copy(f32[32,8]{0,1:T(8,128)} %param.22) | data formatting | bytes 2048 | tf_op args[9]
  3.3 1.4 %copy.18.nbr_hbm = s32[32,6]{1,0:T(8,128)} copy(s32[32,6]{0,1:T(8,128)} %param.23) | data formatting | bytes 1536 | tf_op args[10]
  4.7 1.5 %copy.19.m_idx_hbm = s32[256,4]{1,0:T(8,128)} copy(s32[256,4]{0,1:T(4,128)} %param.24) | data formatting | bytes 8192 | tf_op args[11]
  6.2 1.5 %copy.20.m_w_hbm = f32[256,4]{1,0:T(8,128)} copy(f32[256,4]{0,1:T(4,128)} %param.25) | data formatting | bytes 8192 | tf_op args[12]
  7.7 75.4 %forecast_step.1 = (f32[256,128]{1,0:T(8,128)}, f32[1,128]{1,0:T(1,128)}, f32[512,128]{1,0:T(8,128)}) custom-call(f32[256,512]{1,0:T(8,128)} %grid_hbm.1, f32[256,128]{1,0:T(8,128)} %target_hbm.1, f32[512,512]{1,0:T(8,128)} %w_enc_hbm.1, f32[2,512,512]{2,1,0:T(8,128)} %w_self_hbm.1, f32[2,512,512]{2,1,0:T(8,128)} %w_nbr_hbm.1, f32[512,512]{1,0:T(8,128)} %w_dec_hbm.1, ...), custom_call_target="tpu_custom_call" | custom-call | tf_op jit(solution)/shard_map/forecast_step/pallas_call | solution.py:479
  83.1 1.6 %copy.24 = f32[256,128]{1,0:T(8,128)} copy(f32[256,128]{1,0:T(8,128)} %get-tuple-element.12) | data formatting | bytes 262144
  85.3 1.7 %copy.26 = f32[512,128]{1,0:T(8,128)} copy(f32[512,128]{1,0:T(8,128)} %get-tuple-element.14) | data formatting | bytes 524288

commit v2 on v1

v2 whole, which is shorter than its diff:
```python
import functools

import jax
import jax.numpy as jnp
from jax import lax
from jax.experimental import pallas as pl
from jax.experimental.pallas import tpu as pltpu
from jax.sharding import PartitionSpec as P

BS = 16
L = 2
NZ = 12
EPS = 1e-05
F32 = jnp.float32
BF16 = jnp.bfloat16
MESH = pl.DeviceIdType.MESH


def split(value):
    high = value.astype(BF16)
    low = (value - high.astype(F32)).astype(BF16)
    return high, low


def dot(left, right):
    return jnp.dot(left, right, preferred_element_type=F32)


def mm3(left, right):
    (lh, ll), (rh, rl) = left, right
    rows = lh.shape[0]
    both = dot(jnp.concatenate([lh, ll], axis=0), rh)
    return both[:rows] + (both[rows:] + dot(lh, rl))


def silu(value):
    return value / (1.0 + jnp.exp(-value))


def span(index, size):
    return pl.ds(pl.multiple_of(index * size, size), size)


def program_kernel(
    n_lat,
    n_lon,
    nz,
    grid_hbm,
    target_hbm,
    w_enc_hbm,
    w_self_hbm,
    w_nbr_hbm,
    w_dec_hbm,
    w_out_hbm,
    var_weight,
    g_idx_hbm,
    g_w_hbm,
    nbr_hbm,
    m_idx_hbm,
    m_w_hbm,
    pred_hbm,
    loss_ref,
    grad_hbm,
    grid,
    target,
    w_f32,
    w_out,
    g_idx,
    g_w,
    nbr,
    m_idx,
    m_w,
    m_idx_cols,
    m_w_cols,
    w_bf,
    w_out_bf,
    h_bf,
    h_dec,
    back_bf,
    win0,
    win1,
    win2,
    win3,
    pred,
    grad,
    half,
    s1_src,
    s1,
    s2,
    total,
    st0,
    st1,
    st2,
    in_sem,
    out_sem,
    halo_recv,
    halo_send,
    half_recv,
    part_recv,
    ar_recv,
    ar_send,
):
    lat = lax.axis_index("lat")
    lon = lax.axis_index("lon")
    ny = n_lat // nz
    y = lat // nz
    z = lat % nz
    points, width = grid.shape
    n_var = target.shape[1]
    piece = s2.shape[1]
    nx = n_lon // 2
    x = lon // 2
    core = lon % 2
    x_rows = ny * piece
    half_rows = nx * x_rows
    grid_total = float(points * n_lat * n_lon)

    inner = 1 - 2 * core
    outer = -inner

    def near(lat_step, lon_step):
        return ((lat + lat_step + n_lat) % n_lat, (lon + lon_step + n_lon) % n_lon)

    def at_xy(dx, dy):
        return (((y + dy) % ny) * nz + z, ((x + dx) % nx) * 2 + core)

    def at_z(step):
        return (y * nz + (z + step) % nz, lon)

    def ring(count):
        return sorted(range(count), key=lambda d: (-min(d, count - d), d))

    xy_order = [(dx, dy) for dx in range(nx) for dy in range(ny) if dx or dy]
    xy_order.sort(key=lambda d: -(min(d[0], nx - d[0]) + min(d[1], ny - d[1])))
    z_order = [d for d in ring(nz) if d]

    peers = [near(1, 0), near(-1, 0), near(1, outer), near(-1, outer), near(0, outer), near(0, inner)]
    peers += [at_xy(dx, dy) for dx, dy in xy_order]
    peers += [at_z(d) for d in z_order]

    barrier = pltpu.get_barrier_semaphore()
    for peer in peers:
        pl.semaphore_signal(barrier, inc=1, device_id=peer, device_id_type=MESH)

    def load(source, dest, slot):
        return pltpu.make_async_copy(source, dest, in_sem.at[slot])

    quarter = width // 4
    first = [
        load(w_enc_hbm.at[pl.ds(q * quarter, quarter)], w_f32.at[0, pl.ds(q * quarter, quarter)], q)
        for q in range(4)
    ]
    first += [
        load(grid_hbm.at[pl.ds(q * 128, 128)], grid.at[pl.ds(q * 128, 128)], 4 + q)
        for q in range(points // 128)
    ]
    later = [
        load(nbr_hbm, nbr, 6),
        load(m_idx_hbm, m_idx, 7),
        load(m_w_hbm, m_w, 8),
        load(w_dec_hbm, w_f32.at[1], 9),
        load(w_self_hbm.at[0], w_f32.at[2], 10),
        load(w_nbr_hbm.at[0], w_f32.at[3], 11),
        load(w_self_hbm.at[1], w_f32.at[4], 12),
        load(w_nbr_hbm.at[1], w_f32.at[5], 13),
        load(w_out_hbm, w_out, 14),
        load(target_hbm, target, 15),
        load(g_idx_hbm, g_idx, 16),
        load(g_w_hbm, g_w, 17),
    ]
    for copy in first:
        copy.start()

    def split_weight(which, start=0, count=8):
        def body(step, carry):
            rows = span(step, width // 8)
            high, low = split(w_f32[which, rows, :])
            w_bf[which, 0, rows, :] = high
            w_bf[which, 1, rows, :] = low
            return carry

        lax.fori_loop(start, start + count, body, 0)

    def weight(which):
        return w_bf[which, 0], w_bf[which, 1]

    def locate(index, rows):
        shift = rows.bit_length() - 1
        lon_shift = n_lon.bit_length() - 1
        owner = index >> shift
        within = index & (rows - 1)
        band_slot = (owner >> lon_shift) - lat + 1
        tile_slot = ((owner & (n_lon - 1)) - lon + 1 + n_lon) & (n_lon - 1)
        return ((band_slot * 3 + tile_slot) << shift) + within

    def select(local, factors, columns):
        place = lax.broadcasted_iota(jnp.int32, (local.shape[0], columns), 1)
        chosen = jnp.zeros((local.shape[0], columns), F32)
        for k in range(local.shape[1]):
            value = 1.0 if factors is None else factors[:, k : k + 1]
            chosen = chosen + jnp.where(place == local[:, k : k + 1], value, 0.0)
        return chosen

    def send(win, rows, turn, source, dest, group, peer):
        pltpu.make_async_remote_copy(
            src_ref=win.at[span(source, rows)],
            dst_ref=win.at[span(dest, rows)],
            send_sem=halo_send.at[turn],
            recv_sem=halo_recv.at[turn, group],
            device_id=peer,
            device_id_type=MESH,
        ).start()

    def slot(lat_step, lon_step):
        return (lat_step + 1) * 3 + lon_step + 1

    def halo_start(win, rows, turn):
        for step, group in ((1, 0), (-1, 1)):
            send(win, rows, turn, 4, slot(-step, 0), group, near(step, 0))
        for step in (1, -1):
            send(win, rows, turn, 4, slot(-step, -outer), 2, near(step, outer))
        send(win, rows, turn, 4, slot(0, -outer), 2, near(0, outer))
        send(win, rows, turn, 4, slot(0, -inner), 2, near(0, inner))

    def halo_wait(win, rows, turn, group, count):
        part = win.at[pl.ds(0, count * rows)]
        pltpu.make_async_copy(part, part, halo_recv.at[turn, group]).wait()

    def halo_forward(win, rows, turn):
        for step, group in ((-1, 0), (1, 1)):
            halo_wait(win, rows, turn, group, 1)
            send(win, rows, turn, slot(step, 0), slot(step, -inner), 2, near(0, inner))

    def halo_sent(win, rows, turn):
        part = win.at[pl.ds(0, 8 * rows)]
        pltpu.make_async_copy(part, part, halo_send.at[turn]).wait()

    blocks_dev = points // BS
    mesh_dev = nbr.shape[1]
    for q in range(4):
        first[q].wait()
        split_weight(0, 2 * q, 2)
    for copy in later:
        copy.start()
    for copy in first[4:]:
        copy.wait()

    def encode(step, carry):
        rows = span(step, 128)
        value = grid[rows, :]
        h_one = value + silu(mm3(split(value), weight(0)))
        high, low = split(h_one)
        h_bf[0, rows, :] = high
        h_bf[1, rows, :] = low
        means = jnp.sum(h_one.reshape(128 // BS, BS, width), axis=1) * (1.0 / BS)
        start = pl.multiple_of(4 * blocks_dev + step * (128 // BS), 128 // BS)
        win0[pl.ds(start, 128 // BS), :] = means
        return carry

    lax.fori_loop(0, points // 128, encode, 0)
    pl.semaphore_wait(barrier, len(peers))
    halo_start(win0, blocks_dev, 0)

    later[10].wait()
    later[11].wait()
    g_weights = g_w[...].T
    g_local = locate(g_idx[...].T, blocks_dev)
    g_select = split(select(g_local, g_weights, 9 * blocks_dev))
    g_total = jnp.sum(g_weights, axis=1, keepdims=True)
    later[0].wait()
    a_select = select(locate(nbr[...].T, mesh_dev), None, 9 * mesh_dev).astype(BF16)
    later[4].wait()
    split_weight(2)
    later[5].wait()
    split_weight(3)
    later[3].wait()
    split_weight(1)
    halo_forward(win0, blocks_dev, 0)

    def hidden_part(step, carry):
        rows = span(step, 128)
        h_dec[rows, :] = mm3((h_bf[0, rows, :], h_bf[1, rows, :]), weight(1))
        return carry

    lax.fori_loop(0, points // 128, hidden_part, 0)
    halo_wait(win0, blocks_dev, 0, 2, 6)

    mesh = mm3(g_select, split(win0[...])) / g_total
    wins = (win1, win2, win3)

    def own(win):
        return pl.ds(4 * mesh_dev, mesh_dev)

    for layer in range(L):
        win = wins[layer]
        win[own(win), :] = mesh
        halo_start(win, mesh_dev, layer + 1)
        center = mesh - jnp.mean(mesh, axis=1, keepdims=True)
        spread = jnp.mean(center * center, axis=1, keepdims=True)
        nrm = center / jnp.sqrt(spread + EPS)
        self_part = mm3(split(nrm), weight(2 + 2 * layer))
        halo_forward(win, mesh_dev, layer + 1)
        if layer == 0:
            for ready, which in ((6, 4), (7, 5)):
                later[ready].wait()
                split_weight(which)
        else:
            later[1].wait()
            later[2].wait()

            factors = m_w[...].T
            factors = factors / jnp.sum(factors, axis=1, keepdims=True)
            m_w_cols[...] = factors
            m_idx_cols[...] = locate(m_idx[...].T, mesh_dev)

            def build(step, carry):
                rows = span(step, 64)
                chosen = select(m_idx_cols[rows, :], m_w_cols[rows, :], 9 * mesh_dev)
                high, low = split(chosen)
                back_bf[0, rows, :] = high
                back_bf[1, rows, :] = low
                return carry

            lax.fori_loop(0, points // 64, build, 0)
        halo_wait(win, mesh_dev, layer + 1, 2, 6)
        high, low = split(win[...])
        agg = (dot(a_select, high) + dot(a_select, low)) / float(nbr.shape[0])
        mesh = mesh + silu(self_part + mm3(split(agg), weight(3 + 2 * layer)))

    win3[own(win3), :] = mm3(split(mesh), weight(1))
    halo_start(win3, mesh_dev, 3)
    later[8].wait()
    high, low = split(w_out[...])
    w_out_bf[0] = high
    w_out_bf[1] = low
    halo_forward(win3, mesh_dev, 3)
    later[9].wait()
    power = jnp.sum(target[...] * target[...], axis=0, keepdims=True)
    weights = var_weight[...].astype(F32)
    wsum = jnp.sum(weights, axis=1, keepdims=True)
    halo_wait(win3, mesh_dev, 3, 2, 6)

    table = split(win3[...])
    w_out_parts = (w_out_bf[0], w_out_bf[1])
    err = jnp.zeros((1, n_var), F32)
    for step in range(points // 128):
        rows = pl.ds(step * 128, 128)
        hidden = silu(h_dec[rows, :] + mm3((back_bf[0, rows, :], back_bf[1, rows, :]), table))
        hh, hl = split(hidden)
        out = mm3((hh, hl), w_out_parts)
        pred[rows, :] = out
        resid = out - target[rows, :]
        err = err + jnp.sum(resid * resid, axis=0, keepdims=True)
        part = mm3((hh.T, hl.T), split(resid))
        if step == 0:
            grad[...] = part
        else:
            grad[...] += part
    pred_copy = pltpu.make_async_copy(pred, pred_hbm, out_sem.at[0])
    pred_copy.start()

    def push(source, dest, stage, recv, peer):
        pltpu.make_async_remote_copy(
            src_ref=source,
            dst_ref=dest,
            send_sem=ar_send.at[stage],
            recv_sem=recv,
            device_id=peer,
            device_id_type=MESH,
        ).start()

    def drain(part, sem):
        pltpu.make_async_copy(part, part, sem).wait()

    partner = near(0, inner)
    me = x * ny + y
    keep_row = core * half_rows

    st0[core] = jnp.concatenate([power, err], axis=0)
    push(st0.at[core], st0.at[core], 0, ar_recv.at[0], partner)
    for dx in ring(nx):
        bx = (x + dx) % nx
        rows = pl.ds(pl.multiple_of((1 - core) * half_rows + bx * x_rows, x_rows), x_rows)
        push(grad.at[rows], half.at[span(bx, x_rows)], 1, half_recv.at[bx], partner)

    drain(st0.at[pl.ds(0, 1)], ar_recv.at[0])
    st1[me] = st0[0] + st0[1]
    for dx, dy in xy_order:
        push(st1.at[me], st1.at[me], 2, ar_recv.at[1], at_xy(dx, dy))
    for dx in ring(nx):
        bx = (x + dx) % nx
        drain(half.at[span(bx, x_rows)], half_recv.at[bx])
        rows = pl.ds(pl.multiple_of(keep_row + bx * x_rows, x_rows), x_rows)
        s1_src[span(bx, x_rows), :] = grad[rows, :] + half[span(bx, x_rows), :]
        for dy in ring(ny):
            if dx or dy:
                block = bx * ny + (y + dy) % ny
                push(s1_src.at[span(block, piece)], s1.at[me], 3, ar_recv.at[2], at_xy(dx, dy))
    s1[me] = s1_src[span(me, piece), :]

    others = nx * ny - 1
    drain(st1.at[pl.ds(0, others)], ar_recv.at[1])
    st2[z] = jnp.sum(st1[...], axis=0)
    for d in z_order:
        push(st2.at[z], st2.at[z], 4, ar_recv.at[3], at_z(d))
    drain(s1.at[pl.ds(0, others)], ar_recv.at[2])
    s2[z] = jnp.sum(s1[...], axis=0)
    for d in z_order:
        push(s2.at[z], s2.at[z], 5, ar_recv.at[4], at_z(d))

    drain(st2.at[pl.ds(0, nz - 1)], ar_recv.at[3])
    stats = jnp.sum(st2[...], axis=0)
    scale = stats[0:1] / grid_total + 1e-06
    norm = scale * grid_total * wsum
    loss = jnp.sum(weights * stats[1:2] / norm, axis=1, keepdims=True)
    loss_ref[...] = jnp.broadcast_to(loss, loss_ref.shape)
    coef = 2.0 * weights / norm

    drain(s2.at[pl.ds(0, nz - 1)], ar_recv.at[4])
    mine = pl.ds(pl.multiple_of(keep_row + me * piece, piece), piece)
    total[mine, :] = jnp.sum(s2[...], axis=0) * coef
    for dx, dy in xy_order:
        push(total.at[mine], total.at[mine], 6, part_recv.at[x], at_xy(dx, dy))
    for dx in reversed(ring(nx)):
        bx = (x + dx) % nx
        rows = pl.ds(pl.multiple_of(keep_row + bx * x_rows, x_rows), x_rows)
        count = ny - 1 if dx == 0 else ny
        drain(total.at[pl.ds(0, count * piece)], part_recv.at[bx])
        push(total.at[rows], total.at[rows], 7, ar_recv.at[5], partner)
    drain(total.at[pl.ds(0, half_rows)], ar_recv.at[5])
    grad_copy = pltpu.make_async_copy(total, grad_hbm, out_sem.at[1])
    grad_copy.start()

    halo_sent(win0, blocks_dev, 0)
    for turn, win in enumerate(wins):
        halo_sent(win, mesh_dev, turn + 1)
    drain(st0.at[pl.ds(0, 1)], ar_send.at[0])
    drain(grad.at[pl.ds(0, half_rows)], ar_send.at[1])
    drain(st1.at[pl.ds(0, others)], ar_send.at[2])
    drain(s1.at[pl.ds(0, others)], ar_send.at[3])
    drain(st2.at[pl.ds(0, nz - 1)], ar_send.at[4])
    drain(s2.at[pl.ds(0, nz - 1)], ar_send.at[5])
    drain(total.at[pl.ds(0, others * piece)], ar_send.at[6])
    drain(total.at[pl.ds(0, half_rows)], ar_send.at[7])
    pred_copy.wait()
    grad_copy.wait()


def shards(
    nz,
    grid_in,
    target,
    w_enc,
    w_mix_self,
    w_mix_nbr,
    w_dec,
    w_out,
    var_weight,
    g2m_idx,
    g2m_w,
    mesh_nbr,
    m2g_idx,
    m2g_w,
):
    n_lat = lax.axis_size("lat")
    n_lon = lax.axis_size("lon")
    ny = n_lat // nz
    points, width = grid_in.shape
    n_var = target.shape[1]
    mesh_dev = mesh_nbr.shape[0]
    turned = (g2m_idx.T, g2m_w.T, mesh_nbr.T, m2g_idx.T, m2g_w.T)
    blocks_dev = points // BS
    piece = width // (n_lon * ny)
    window = 9 * mesh_dev
    hbm = pl.BlockSpec(memory_space=pl.ANY)
    vmem = pl.BlockSpec(memory_space=pltpu.VMEM)
    pred, loss, grad = pl.pallas_call(
        functools.partial(program_kernel, n_lat, n_lon, nz),
        name="forecast_step",
        out_shape=(
            jax.ShapeDtypeStruct((points, n_var), F32),
            jax.ShapeDtypeStruct((1, n_var), F32),
            jax.ShapeDtypeStruct((width, n_var), F32),
        ),
        in_specs=[hbm] * 7 + [vmem] + [hbm] * 5,
        out_specs=(hbm, vmem, hbm),
        scratch_shapes=[
            pltpu.VMEM((points, width), F32),
            pltpu.VMEM((points, n_var), F32),
            pltpu.VMEM((6, width, width), F32),
            pltpu.VMEM((width, n_var), F32),
            *[pltpu.VMEM(a.shape, a.dtype) for a in turned],
            pltpu.VMEM(m2g_idx.shape, jnp.int32),
            pltpu.VMEM(m2g_w.shape, F32),
            pltpu.VMEM((6, 2, width, width), BF16),
            pltpu.VMEM((2, width, n_var), BF16),
            pltpu.VMEM((2, points, width), BF16),
            pltpu.VMEM((points, width), F32),
            pltpu.VMEM((2, points, window), BF16),
            pltpu.VMEM((9 * blocks_dev, width), F32),
            pltpu.VMEM((window, width), F32),
            pltpu.VMEM((window, width), F32),
            pltpu.VMEM((window, width), F32),
            pltpu.VMEM((points, n_var), F32),
            pltpu.VMEM((width, n_var), F32),
            pltpu.VMEM((width // 2, n_var), F32),
            pltpu.VMEM((width // 2, n_var), F32),
            pltpu.VMEM((n_lon // 2 * ny, piece, n_var), F32),
            pltpu.VMEM((nz, piece, n_var), F32),
            pltpu.VMEM((width, n_var), F32),
            pltpu.VMEM((2, 2, n_var), F32),
            pltpu.VMEM((n_lon // 2 * ny, 2, n_var), F32),
            pltpu.VMEM((nz, 2, n_var), F32),
            pltpu.SemaphoreType.DMA((18,)),
            pltpu.SemaphoreType.DMA((2,)),
            pltpu.SemaphoreType.DMA((4, 3)),
            pltpu.SemaphoreType.DMA((4,)),
            pltpu.SemaphoreType.DMA((n_lon // 2,)),
            pltpu.SemaphoreType.DMA((n_lon // 2,)),
            pltpu.SemaphoreType.DMA((6,)),
            pltpu.SemaphoreType.DMA((8,)),
        ],
        compiler_params=pltpu.CompilerParams(collective_id=0, has_side_effects=True),
    )(
        grid_in,
        target,
        w_enc,
        w_mix_self,
        w_mix_nbr,
        w_dec,
        w_out,
        var_weight.reshape(1, n_var),
        *turned,
    )
    return (pred, loss[0, 0], grad)


def solution(mesh, nz=NZ):
    rows = P(("lat", "lon"), None)
    placed = (rows, rows, P(), P(), P(), P(), P(), P(), rows, rows, rows, rows, rows)
    return jax.shard_map(
        functools.partial(shards, nz),
        mesh=mesh,
        in_specs=placed,
        out_specs=(rows, P(), P()),
        check_vma=False,
    )
```

time: 88.5 us -> 76.6 us (0.87)
  local copies, waits for them, and re-layouts: 10.3 us -> 3.24 us
  Pallas kernels: 75.4 us -> 70.7 us
    unnamed x7 -> x2, local copies, waits for them, and re-layouts: 10.3 us -> 3.24 us
    pallas_call x1, Pallas kernels: 75.4 us -> 70.7 us  [shards(): pl.pallas_call(functools.partial(program_kernel, n_lat, n_lon, nz), name=...]
where the time goes in v2:
time: 76.6 us; the launch traced here: 76.3 us
  Pallas kernels  70.7 us (92%)
  local copies, waits for them, and re-layouts  3.24 us (4%)
  between operations  2.4 us (3%)
    pallas_call x1, Pallas kernels, shards(): pl.pallas_call(functools.partial(program_kernel, n_lat, n_lon, nz), name=...  70.7 us
    unnamed x2, local copies, waits for them, and re-layouts  3.24 us

profile of v2, /device:TPU:1, one launch (start us, length us, event | category | flops | bytes accessed | tf_op | source)
XLA Modules:
  0.0 76.3 jit_solution(12892844247053741046)
XLA Ops:
  0.6 70.7 %forecast_step.1 = (f32[256,128]{1,0:T(8,128)}, f32[1,128]{1,0:T(1,128)}, f32[512,128]{1,0:T(8,128)}) custom-call(f32[256,512]{1,0:T(8,128)} %grid_hbm.1, f32[256,128]{1,0:T(8,128)} %target_hbm.1, f32[512,512]{1,0:T(8,128)} %w_enc_hbm.1, f32[2,512,512]{2,1,0:T(8,128)} %w_self_hbm.1, f32[2,512,512]{2,1,0:T(8,128)} %w_nbr_hbm.1, f32[512,512]{1,0:T(8,128)} %w_dec_hbm.1, ...), custom_call_target="tpu_custom_call" | custom-call | tf_op jit(solution)/shard_map/forecast_step/pallas_call | solution.py:477
  71.3 1.6 %copy.19 = f32[256,128]{1,0:T(8,128)} copy(f32[256,128]{1,0:T(8,128)} %get-tuple-element.12) | data formatting | bytes 262144
  73.5 1.7 %copy.21 = f32[512,128]{1,0:T(8,128)} copy(f32[512,128]{1,0:T(8,128)} %get-tuple-element.14) | data formatting | bytes 524288

commit v3 on v2

--- a/solution.py
+++ b/solution.py
@@ -39,6 +39,10 @@
 
 def span(index, size):
     return pl.ds(pl.multiple_of(index * size, size), size)
+
+
+def lanes(count):
+    return -(-count // 128) * 128
 
 
 def program_kernel(
@@ -52,19 +56,20 @@
     w_nbr_hbm,
     w_dec_hbm,
     w_out_hbm,
-    var_weight,
+    vw_hbm,
     g_idx_hbm,
     g_w_hbm,
     nbr_hbm,
     m_idx_hbm,
     m_w_hbm,
-    pred_hbm,
-    loss_ref,
-    grad_hbm,
+    pred_out,
+    loss_out,
+    grad_out,
     grid,
     target,
     w_f32,
     w_out,
+    vw,
     g_idx,
     g_w,
     nbr,
@@ -87,7 +92,8 @@
     s1_src,
     s1,
     s2,
-    total,
+    done,
+    loss_row,
     st0,
     st1,
     st2,
@@ -167,6 +173,7 @@
         load(target_hbm, target, 15),
         load(g_idx_hbm, g_idx, 16),
         load(g_w_hbm, g_w, 17),
+        load(vw_hbm, vw, 18),
     ]
     for copy in first:
         copy.start()
@@ -191,7 +198,10 @@
         within = index & (rows - 1)
         band_slot = (owner >> lon_shift) - lat + 1
         tile_slot = ((owner & (n_lon - 1)) - lon + 1 + n_lon) & (n_lon - 1)
-        return ((band_slot * 3 + tile_slot) << shift) + within
+        lone = jnp.where(tile_slot == 1, 0, 1 + (tile_slot >> 1))
+        other = jnp.where(tile_slot == 1, 3 + (band_slot >> 1), (band_slot & 2) + (tile_slot >> 1))
+        far = jnp.where((band_slot == 1) | (tile_slot == 1), 0, lanes(5 * rows))
+        return (jnp.where(band_slot == 1, lone, other) << shift) + within + far
 
     def select(local, factors, columns):
         place = lax.broadcasted_iota(jnp.int32, (local.shape[0], columns), 1)
@@ -211,25 +221,42 @@
             device_id_type=MESH,
         ).start()
 
-    def slot(lat_step, lon_step):
-        return (lat_step + 1) * 3 + lon_step + 1
+    def lon_slot(step):
+        return 1 + (step + 1) // 2
+
+    def lat_slot(step):
+        return 3 + (step + 1) // 2
+
+    def corner(lat_step, lon_step):
+        return 5 + (lat_step + 1) + (lon_step + 1) // 2
 
     def halo_start(win, rows, turn):
-        for step, group in ((1, 0), (-1, 1)):
-            send(win, rows, turn, 4, slot(-step, 0), group, near(step, 0))
         for step in (1, -1):
-            send(win, rows, turn, 4, slot(-step, -outer), 2, near(step, outer))
-        send(win, rows, turn, 4, slot(0, -outer), 2, near(0, outer))
-        send(win, rows, turn, 4, slot(0, -inner), 2, near(0, inner))
+            send(win, rows, turn, 0, lat_slot(-step), lat_slot(-step) - 2, near(step, 0))
+        for step in (1, -1):
+            send(win, rows, turn, 0, corner(-step, -outer), 3, near(step, outer))
+        send(win, rows, turn, 0, lon_slot(-outer), 0, near(0, outer))
+        send(win, rows, turn, 0, lon_slot(-inner), 0, near(0, inner))
 
     def halo_wait(win, rows, turn, group, count):
         part = win.at[pl.ds(0, count * rows)]
         pltpu.make_async_copy(part, part, halo_recv.at[turn, group]).wait()
 
     def halo_forward(win, rows, turn):
-        for step, group in ((-1, 0), (1, 1)):
-            halo_wait(win, rows, turn, group, 1)
-            send(win, rows, turn, slot(step, 0), slot(step, -inner), 2, near(0, inner))
+        for step in (-1, 1):
+            halo_wait(win, rows, turn, lat_slot(step) - 2, 1)
+            send(win, rows, turn, lat_slot(step), corner(step, -inner), 3, near(0, inner))
+
+    def halo_inner(win, rows, turn):
+        halo_wait(win, rows, turn, 0, 2)
+        return split(win[0 : 5 * rows, :])
+
+    def halo_corners(win, rows, turn):
+        halo_wait(win, rows, turn, 3, 4)
+        return split(win[5 * rows : 9 * rows, :])
+
+    def columns(parts, start, stop):
+        return tuple(part[:, start:stop] for part in parts)
 
     def halo_sent(win, rows, turn):
         part = win.at[pl.ds(0, 8 * rows)]
@@ -253,7 +280,7 @@
         h_bf[0, rows, :] = high
         h_bf[1, rows, :] = low
         means = jnp.sum(h_one.reshape(128 // BS, BS, width), axis=1) * (1.0 / BS)
-        start = pl.multiple_of(4 * blocks_dev + step * (128 // BS), 128 // BS)
+        start = pl.multiple_of(step * (128 // BS), 128 // BS)
         win0[pl.ds(start, 128 // BS), :] = means
         return carry
 
@@ -265,31 +292,36 @@
     later[11].wait()
     g_weights = g_w[...].T
     g_local = locate(g_idx[...].T, blocks_dev)
-    g_select = split(select(g_local, g_weights, 9 * blocks_dev))
+    g_far = lanes(5 * blocks_dev)
+    g_select = split(select(g_local, g_weights, g_far + 4 * blocks_dev))
     g_total = jnp.sum(g_weights, axis=1, keepdims=True)
     later[0].wait()
-    a_select = select(locate(nbr[...].T, mesh_dev), None, 9 * mesh_dev).astype(BF16)
+    far = lanes(5 * mesh_dev)
+    a_select = select(locate(nbr[...].T, mesh_dev), None, far + 4 * mesh_dev).astype(BF16)
     later[4].wait()
     split_weight(2)
     later[5].wait()
     split_weight(3)
-    later[3].wait()
-    split_weight(1)
     halo_forward(win0, blocks_dev, 0)
+    cut = 5 * blocks_dev
+    mesh = mm3(columns(g_select, 0, cut), halo_inner(win0, blocks_dev, 0))
+    mesh = mesh + mm3(columns(g_select, g_far, g_far + 4 * blocks_dev), halo_corners(win0, blocks_dev, 0))
+    mesh = mesh / g_total
 
     def hidden_part(step, carry):
         rows = span(step, 128)
         h_dec[rows, :] = mm3((h_bf[0, rows, :], h_bf[1, rows, :]), weight(1))
         return carry
 
-    lax.fori_loop(0, points // 128, hidden_part, 0)
-    halo_wait(win0, blocks_dev, 0, 2, 6)
-
-    mesh = mm3(g_select, split(win0[...])) / g_total
+    def gather(parts):
+        high, low = parts[1]
+        return dot(parts[0], high) + dot(parts[0], low)
+
+    cut = 5 * mesh_dev
     wins = (win1, win2, win3)
 
     def own(win):
-        return pl.ds(4 * mesh_dev, mesh_dev)
+        return pl.ds(0, mesh_dev)
 
     for layer in range(L):
         win = wins[layer]
@@ -299,32 +331,34 @@
         spread = jnp.mean(center * center, axis=1, keepdims=True)
         nrm = center / jnp.sqrt(spread + EPS)
         self_part = mm3(split(nrm), weight(2 + 2 * layer))
-        halo_forward(win, mesh_dev, layer + 1)
         if layer == 0:
             for ready, which in ((6, 4), (7, 5)):
                 later[ready].wait()
                 split_weight(which)
-        else:
+            later[3].wait()
+            split_weight(1)
+            halo_forward(win, mesh_dev, layer + 1)
             later[1].wait()
             later[2].wait()
-
             factors = m_w[...].T
-            factors = factors / jnp.sum(factors, axis=1, keepdims=True)
-            m_w_cols[...] = factors
+            m_w_cols[...] = factors / jnp.sum(factors, axis=1, keepdims=True)
             m_idx_cols[...] = locate(m_idx[...].T, mesh_dev)
 
             def build(step, carry):
                 rows = span(step, 64)
-                chosen = select(m_idx_cols[rows, :], m_w_cols[rows, :], 9 * mesh_dev)
+                chosen = select(m_idx_cols[rows, :], m_w_cols[rows, :], far + 4 * mesh_dev)
                 high, low = split(chosen)
                 back_bf[0, rows, :] = high
                 back_bf[1, rows, :] = low
                 return carry
 
             lax.fori_loop(0, points // 64, build, 0)
-        halo_wait(win, mesh_dev, layer + 1, 2, 6)
-        high, low = split(win[...])
-        agg = (dot(a_select, high) + dot(a_select, low)) / float(nbr.shape[0])
+        else:
+            lax.fori_loop(0, points // 128, hidden_part, 0)
+            halo_forward(win, mesh_dev, layer + 1)
+        agg = gather((a_select[:, :cut], halo_inner(win, mesh_dev, layer + 1)))
+        agg = agg + gather((a_select[:, far:], halo_corners(win, mesh_dev, layer + 1)))
+        agg = agg / float(nbr.shape[0])
         mesh = mesh + silu(self_part + mm3(split(agg), weight(3 + 2 * layer)))
 
     win3[own(win3), :] = mm3(split(mesh), weight(1))
@@ -336,16 +370,20 @@
     halo_forward(win3, mesh_dev, 3)
     later[9].wait()
     power = jnp.sum(target[...] * target[...], axis=0, keepdims=True)
-    weights = var_weight[...].astype(F32)
+    later[12].wait()
+    weights = vw[...].astype(F32)
     wsum = jnp.sum(weights, axis=1, keepdims=True)
-    halo_wait(win3, mesh_dev, 3, 2, 6)
-
-    table = split(win3[...])
+    table = halo_inner(win3, mesh_dev, 3)
+    for step in range(points // 128):
+        rows = pl.ds(step * 128, 128)
+        h_dec[rows, :] += mm3((back_bf[0, rows, 0:cut], back_bf[1, rows, 0:cut]), table)
+    table = halo_corners(win3, mesh_dev, 3)
     w_out_parts = (w_out_bf[0], w_out_bf[1])
     err = jnp.zeros((1, n_var), F32)
     for step in range(points // 128):
         rows = pl.ds(step * 128, 128)
-        hidden = silu(h_dec[rows, :] + mm3((back_bf[0, rows, :], back_bf[1, rows, :]), table))
+        corners = (back_bf[0, rows, pl.ds(far, 4 * mesh_dev)], back_bf[1, rows, pl.ds(far, 4 * mesh_dev)])
+        hidden = silu(h_dec[rows, :] + mm3(corners, table))
         hh, hl = split(hidden)
         out = mm3((hh, hl), w_out_parts)
         pred[rows, :] = out
@@ -356,7 +394,7 @@
             grad[...] = part
         else:
             grad[...] += part
-    pred_copy = pltpu.make_async_copy(pred, pred_hbm, out_sem.at[0])
+    pred_copy = pltpu.make_async_copy(pred, pred_out, out_sem.at[0])
     pred_copy.start()
 
     def push(source, dest, stage, recv, peer):
@@ -413,23 +451,26 @@
     scale = stats[0:1] / grid_total + 1e-06
     norm = scale * grid_total * wsum
     loss = jnp.sum(weights * stats[1:2] / norm, axis=1, keepdims=True)
-    loss_ref[...] = jnp.broadcast_to(loss, loss_ref.shape)
+    loss_row[...] = jnp.broadcast_to(loss, loss_row.shape)
+    loss_copy = pltpu.make_async_copy(loss_row, loss_out, out_sem.at[1])
+    loss_copy.start()
     coef = 2.0 * weights / norm
 
     drain(s2.at[pl.ds(0, nz - 1)], ar_recv.at[4])
     mine = pl.ds(pl.multiple_of(keep_row + me * piece, piece), piece)
-    total[mine, :] = jnp.sum(s2[...], axis=0) * coef
+    done[...] = jnp.sum(s2[...], axis=0) * coef
     for dx, dy in xy_order:
-        push(total.at[mine], total.at[mine], 6, part_recv.at[x], at_xy(dx, dy))
+        push(done, grad_out.at[mine], 6, part_recv.at[x], at_xy(dx, dy))
+    done_copy = pltpu.make_async_copy(done, grad_out.at[mine], out_sem.at[2])
+    done_copy.start()
+    done_copy.wait()
     for dx in reversed(ring(nx)):
         bx = (x + dx) % nx
         rows = pl.ds(pl.multiple_of(keep_row + bx * x_rows, x_rows), x_rows)
         count = ny - 1 if dx == 0 else ny
-        drain(total.at[pl.ds(0, count * piece)], part_recv.at[bx])
-        push(total.at[rows], total.at[rows], 7, ar_recv.at[5], partner)
-    drain(total.at[pl.ds(0, half_rows)], ar_recv.at[5])
-    grad_copy = pltpu.make_async_copy(total, grad_hbm, out_sem.at[1])
-    grad_copy.start()
+        drain(grad_out.at[pl.ds(0, count * piece)], part_recv.at[bx])
+        push(grad_out.at[rows], grad_out.at[rows], 7, ar_recv.at[5], partner)
+    drain(grad_out.at[pl.ds(0, half_rows)], ar_recv.at[5])
 
     halo_sent(win0, blocks_dev, 0)
     for turn, win in enumerate(wins):
@@ -440,10 +481,10 @@
     drain(s1.at[pl.ds(0, others)], ar_send.at[3])
     drain(st2.at[pl.ds(0, nz - 1)], ar_send.at[4])
     drain(s2.at[pl.ds(0, nz - 1)], ar_send.at[5])
-    drain(total.at[pl.ds(0, others * piece)], ar_send.at[6])
-    drain(total.at[pl.ds(0, half_rows)], ar_send.at[7])
+    drain(s1.at[pl.ds(0, others)], ar_send.at[6])
+    drain(grad_out.at[pl.ds(0, half_rows)], ar_send.at[7])
     pred_copy.wait()
-    grad_copy.wait()
+    loss_copy.wait()
 
 
 def shards(
@@ -472,8 +513,9 @@
     blocks_dev = points // BS
     piece = width // (n_lon * ny)
     window = 9 * mesh_dev
+    vw = var_weight.reshape(1, n_var)
+    operands = (grid_in, target, w_enc, w_mix_self, w_mix_nbr, w_dec, w_out, vw, *turned)
     hbm = pl.BlockSpec(memory_space=pl.ANY)
-    vmem = pl.BlockSpec(memory_space=pltpu.VMEM)
     pred, loss, grad = pl.pallas_call(
         functools.partial(program_kernel, n_lat, n_lon, nz),
         name="forecast_step",
@@ -482,13 +524,14 @@
             jax.ShapeDtypeStruct((1, n_var), F32),
             jax.ShapeDtypeStruct((width, n_var), F32),
         ),
-        in_specs=[hbm] * 7 + [vmem] + [hbm] * 5,
-        out_specs=(hbm, vmem, hbm),
+        in_specs=[hbm] * len(operands),
+        out_specs=(hbm, hbm, hbm),
         scratch_shapes=[
             pltpu.VMEM((points, width), F32),
             pltpu.VMEM((points, n_var), F32),
             pltpu.VMEM((6, width, width), F32),
             pltpu.VMEM((width, n_var), F32),
+            pltpu.VMEM((1, n_var), jnp.int32),
             *[pltpu.VMEM(a.shape, a.dtype) for a in turned],
             pltpu.VMEM(m2g_idx.shape, jnp.int32),
             pltpu.VMEM(m2g_w.shape, F32),
@@ -496,7 +539,7 @@
             pltpu.VMEM((2, width, n_var), BF16),
             pltpu.VMEM((2, points, width), BF16),
             pltpu.VMEM((points, width), F32),
-            pltpu.VMEM((2, points, window), BF16),
+            pltpu.VMEM((2, points, lanes(5 * mesh_dev) + 4 * mesh_dev), BF16),
             pltpu.VMEM((9 * blocks_dev, width), F32),
             pltpu.VMEM((window, width), F32),
             pltpu.VMEM((window, width), F32),
@@ -507,31 +550,24 @@
             pltpu.VMEM((width // 2, n_var), F32),
             pltpu.VMEM((n_lon // 2 * ny, piece, n_var), F32),
             pltpu.VMEM((nz, piece, n_var), F32),
-            pltpu.VMEM((width, n_var), F32),
+            pltpu.VMEM((piece, n_var), F32),
+            pltpu.VMEM((1, n_var), F32),
             pltpu.VMEM((2, 2, n_var), F32),
             pltpu.VMEM((n_lon // 2 * ny, 2, n_var), F32),
             pltpu.VMEM((nz, 2, n_var), F32),
-            pltpu.SemaphoreType.DMA((18,)),
-            pltpu.SemaphoreType.DMA((2,)),
-            pltpu.SemaphoreType.DMA((4, 3)),
+            pltpu.SemaphoreType.DMA((19,)),
+            pltpu.SemaphoreType.DMA((3,)),
+            pltpu.SemaphoreType.DMA((4, 4)),
             pltpu.SemaphoreType.DMA((4,)),
             pltpu.SemaphoreType.DMA((n_lon // 2,)),
             pltpu.SemaphoreType.DMA((n_lon // 2,)),
             pltpu.SemaphoreType.DMA((6,)),
             pltpu.SemaphoreType.DMA((8,)),
         ],
-        compiler_params=pltpu.CompilerParams(collective_id=0, has_side_effects=True),
-    )(
-        grid_in,
-        target,
-        w_enc,
-        w_mix_self,
-        w_mix_nbr,
-        w_dec,
-        w_out,
-        var_weight.reshape(1, n_var),
-        *turned,
-    )
+        compiler_params=pltpu.CompilerParams(
+            collective_id=0, has_side_effects=True, vmem_limit_bytes=28 << 20
+        ),
+    )(*[pltpu.with_memory_space_constraint(a, pltpu.HBM) for a in operands])
     return (pred, loss[0, 0], grad)
 
 

time: 76.6 us -> 71.1 us (0.928)
  Pallas kernels: 70.7 us -> 67.8 us
  local copies, waits for them, and re-layouts: 3.24 us -> 1.36 us
    pallas_call x1, Pallas kernels: 70.7 us -> 67.8 us  [shards(): pl.pallas_call(functools.partial(program_kernel, n_lat, n_lon, nz), name=...]
    unnamed x2, local copies, waits for them, and re-layouts: 3.24 us -> 1.36 us
where the time goes in v3:
time: 71.1 us; the launch traced here: 70.9 us
  Pallas kernels  67.8 us (95%)
  between operations  1.81 us (3%)
  local copies, waits for them, and re-layouts  1.36 us (2%)
    pallas_call x1, Pallas kernels, shards(): pl.pallas_call(functools.partial(program_kernel, n_lat, n_lon, nz), name=...  67.8 us

profile of v3, /device:TPU:1, one launch (start us, length us, event | category | flops | bytes accessed | tf_op | source)
XLA Modules:
  0.0 70.9 jit_solution(11740013555917797018)
XLA Ops:
  0.6 67.8 %forecast_step.1 = (f32[256,128]{1,0:T(8,128)S(1)}, f32[1,128]{1,0:T(1,128)S(1)}, f32[512,128]{1,0:T(8,128)S(1)}) custom-call(f32[256,512]{1,0:T(8,128)} %grid_hbm.1, f32[256,128]{1,0:T(8,128)} %target_hbm.1, f32[512,512]{1,0:T(8,128)} %w_enc_hbm.1, f32[2,512,512]{2,1,0:T(8,128)} %w_self_hbm.1, f32[2,512,512]{2,1,0:T(8,128)} %w_nbr_hbm.1, ...), custom_call_target="tpu_custom_call" | custom-call | tf_op jit(solution)/shard_map/forecast_step/pallas_call | solution.py:519
  68.4 0.7 copy.19
  69.1 0.7 copy.21

commit v4 on v3

--- a/solution.py
+++ b/solution.py
@@ -43,6 +43,17 @@
 
 def lanes(count):
     return -(-count // 128) * 128
+
+
+def place_kernel(pred_in, grad_in, pred_out, grad_out, sem):
+    copies = [
+        pltpu.make_async_copy(grad_in, grad_out, sem.at[0]),
+        pltpu.make_async_copy(pred_in, pred_out, sem.at[1]),
+    ]
+    for copy in copies:
+        copy.start()
+    for copy in copies:
+        copy.wait()
 
 
 def program_kernel(
@@ -80,6 +91,7 @@
     w_bf,
     w_out_bf,
     h_bf,
+    resid_bf,
     h_dec,
     back_bf,
     win0,
@@ -95,8 +107,6 @@
     done,
     loss_row,
     st0,
-    st1,
-    st2,
     in_sem,
     out_sem,
     halo_recv,
@@ -113,7 +123,7 @@
     z = lat % nz
     points, width = grid.shape
     n_var = target.shape[1]
-    piece = s2.shape[1]
+    piece = done.shape[0]
     nx = n_lon // 2
     x = lon // 2
     core = lon % 2
@@ -124,14 +134,27 @@
     inner = 1 - 2 * core
     outer = -inner
 
-    def near(lat_step, lon_step):
-        return ((lat + lat_step + n_lat) % n_lat, (lon + lon_step + n_lon) % n_lon)
+    def wrap(value, count):
+        value = jnp.where(value >= count, value - count, value)
+        return jnp.where(value < 0, value + count, value)
+
+    lats = {step: wrap(lat + step, n_lat) for step in (-1, 0, 1)}
+    xs = [wrap(x + step, nx) for step in range(nx)]
+    ys = [wrap(y + step, ny) for step in range(ny)]
+    y_lats = [value * nz + z for value in ys]
+    x_lons = [value * 2 + core for value in xs]
+    z_lats = [y * nz + wrap(z + step, nz) for step in range(nz)]
+    inner_lon = lon + inner
+    outer_lon = wrap(lon + outer, n_lon)
+
+    def near(lat_step, to_lon):
+        return (lats[lat_step], to_lon)
 
     def at_xy(dx, dy):
-        return (((y + dy) % ny) * nz + z, ((x + dx) % nx) * 2 + core)
+        return (y_lats[dy], x_lons[dx])
 
     def at_z(step):
-        return (y * nz + (z + step) % nz, lon)
+        return (z_lats[step], lon)
 
     def ring(count):
         return sorted(range(count), key=lambda d: (-min(d, count - d), d))
@@ -140,13 +163,10 @@
     xy_order.sort(key=lambda d: -(min(d[0], nx - d[0]) + min(d[1], ny - d[1])))
     z_order = [d for d in ring(nz) if d]
 
-    peers = [near(1, 0), near(-1, 0), near(1, outer), near(-1, outer), near(0, outer), near(0, inner)]
+    peers = [near(step, to) for step in (1, -1) for to in (lon, outer_lon)]
+    peers += [near(0, outer_lon), near(0, inner_lon)]
     peers += [at_xy(dx, dy) for dx, dy in xy_order]
     peers += [at_z(d) for d in z_order]
-
-    barrier = pltpu.get_barrier_semaphore()
-    for peer in peers:
-        pl.semaphore_signal(barrier, inc=1, device_id=peer, device_id_type=MESH)
 
     def load(source, dest, slot):
         return pltpu.make_async_copy(source, dest, in_sem.at[slot])
@@ -178,6 +198,10 @@
     for copy in first:
         copy.start()
 
+    barrier = pltpu.get_barrier_semaphore()
+    for peer in peers:
+        pl.semaphore_signal(barrier, inc=1, device_id=peer, device_id_type=MESH)
+
     def split_weight(which, start=0, count=8):
         def body(step, carry):
             rows = span(step, width // 8)
@@ -232,11 +256,11 @@
 
     def halo_start(win, rows, turn):
         for step in (1, -1):
-            send(win, rows, turn, 0, lat_slot(-step), lat_slot(-step) - 2, near(step, 0))
+            send(win, rows, turn, 0, lat_slot(-step), lat_slot(-step) - 2, near(step, lon))
         for step in (1, -1):
-            send(win, rows, turn, 0, corner(-step, -outer), 3, near(step, outer))
-        send(win, rows, turn, 0, lon_slot(-outer), 0, near(0, outer))
-        send(win, rows, turn, 0, lon_slot(-inner), 0, near(0, inner))
+            send(win, rows, turn, 0, corner(-step, -outer), 3, near(step, outer_lon))
+        send(win, rows, turn, 0, lon_slot(-outer), 0, near(0, outer_lon))
+        send(win, rows, turn, 0, lon_slot(-inner), 0, near(0, inner_lon))
 
     def halo_wait(win, rows, turn, group, count):
         part = win.at[pl.ds(0, count * rows)]
@@ -245,7 +269,7 @@
     def halo_forward(win, rows, turn):
         for step in (-1, 1):
             halo_wait(win, rows, turn, lat_slot(step) - 2, 1)
-            send(win, rows, turn, lat_slot(step), corner(step, -inner), 3, near(0, inner))
+            send(win, rows, turn, lat_slot(step), corner(step, -inner), 3, near(0, inner_lon))
 
     def halo_inner(win, rows, turn):
         halo_wait(win, rows, turn, 0, 2)
@@ -389,13 +413,17 @@
         pred[rows, :] = out
         resid = out - target[rows, :]
         err = err + jnp.sum(resid * resid, axis=0, keepdims=True)
-        part = mm3((hh.T, hl.T), split(resid))
-        if step == 0:
-            grad[...] = part
-        else:
-            grad[...] += part
-    pred_copy = pltpu.make_async_copy(pred, pred_out, out_sem.at[0])
-    pred_copy.start()
+        h_bf[0, rows, :] = hh
+        h_bf[1, rows, :] = hl
+        high, low = split(resid)
+        resid_bf[0, rows, :] = high
+        resid_bf[1, rows, :] = low
+
+    def grad_half(start):
+        rows = pl.ds(pl.multiple_of(start, half_rows), half_rows)
+        left = (h_bf[0, :, rows].T, h_bf[1, :, rows].T)
+        grad[rows, :] = mm3(left, (resid_bf[0], resid_bf[1]))
+        return rows
 
     def push(source, dest, stage, recv, peer):
         pltpu.make_async_remote_copy(
@@ -410,79 +438,67 @@
     def drain(part, sem):
         pltpu.make_async_copy(part, part, sem).wait()
 
-    partner = near(0, inner)
+    partner = near(0, inner_lon)
     me = x * ny + y
     keep_row = core * half_rows
 
     st0[core] = jnp.concatenate([power, err], axis=0)
     push(st0.at[core], st0.at[core], 0, ar_recv.at[0], partner)
-    for dx in ring(nx):
-        bx = (x + dx) % nx
-        rows = pl.ds(pl.multiple_of((1 - core) * half_rows + bx * x_rows, x_rows), x_rows)
-        push(grad.at[rows], half.at[span(bx, x_rows)], 1, half_recv.at[bx], partner)
+    given = grad_half((1 - core) * half_rows)
+    push(grad.at[given], half, 1, half_recv.at[0], partner)
+    kept = grad_half(keep_row)
+    pred_copy = pltpu.make_async_copy(pred, pred_out, out_sem.at[0])
+    pred_copy.start()
 
     drain(st0.at[pl.ds(0, 1)], ar_recv.at[0])
-    st1[me] = st0[0] + st0[1]
+    s1_src[:, piece : piece + 2, :] = jnp.broadcast_to((st0[0] + st0[1])[None], (nx * ny, 2, n_var))
+    drain(half, half_recv.at[0])
+    s1_src[:, 0:piece, :] = (grad[kept, :] + half[...]).reshape(nx * ny, piece, n_var)
     for dx, dy in xy_order:
-        push(st1.at[me], st1.at[me], 2, ar_recv.at[1], at_xy(dx, dy))
-    for dx in ring(nx):
-        bx = (x + dx) % nx
-        drain(half.at[span(bx, x_rows)], half_recv.at[bx])
-        rows = pl.ds(pl.multiple_of(keep_row + bx * x_rows, x_rows), x_rows)
-        s1_src[span(bx, x_rows), :] = grad[rows, :] + half[span(bx, x_rows), :]
-        for dy in ring(ny):
-            if dx or dy:
-                block = bx * ny + (y + dy) % ny
-                push(s1_src.at[span(block, piece)], s1.at[me], 3, ar_recv.at[2], at_xy(dx, dy))
-    s1[me] = s1_src[span(me, piece), :]
+        push(s1_src.at[xs[dx] * ny + ys[dy]], s1.at[me], 2, ar_recv.at[1], at_xy(dx, dy))
+    s1[me] = s1_src[me]
 
     others = nx * ny - 1
-    drain(st1.at[pl.ds(0, others)], ar_recv.at[1])
-    st2[z] = jnp.sum(st1[...], axis=0)
-    for d in z_order:
-        push(st2.at[z], st2.at[z], 4, ar_recv.at[3], at_z(d))
-    drain(s1.at[pl.ds(0, others)], ar_recv.at[2])
+    drain(s1.at[pl.ds(0, others)], ar_recv.at[1])
     s2[z] = jnp.sum(s1[...], axis=0)
     for d in z_order:
-        push(s2.at[z], s2.at[z], 5, ar_recv.at[4], at_z(d))
-
-    drain(st2.at[pl.ds(0, nz - 1)], ar_recv.at[3])
-    stats = jnp.sum(st2[...], axis=0)
+        push(s2.at[z], s2.at[z], 3, ar_recv.at[2], at_z(d))
+
+    drain(s2.at[pl.ds(0, nz - 1)], ar_recv.at[2])
+    value = jnp.sum(s2[...], axis=0)
+    stats = value[piece : piece + 2]
     scale = stats[0:1] / grid_total + 1e-06
     norm = scale * grid_total * wsum
+    coef = 2.0 * weights / norm
+
+    mine = pl.ds(pl.multiple_of(keep_row + me * piece, piece), piece)
+    done[...] = value[0:piece] * coef
+    for dx, dy in xy_order:
+        push(done, grad_out.at[mine], 4, part_recv.at[x], at_xy(dx, dy))
     loss = jnp.sum(weights * stats[1:2] / norm, axis=1, keepdims=True)
     loss_row[...] = jnp.broadcast_to(loss, loss_row.shape)
     loss_copy = pltpu.make_async_copy(loss_row, loss_out, out_sem.at[1])
     loss_copy.start()
-    coef = 2.0 * weights / norm
-
-    drain(s2.at[pl.ds(0, nz - 1)], ar_recv.at[4])
-    mine = pl.ds(pl.multiple_of(keep_row + me * piece, piece), piece)
-    done[...] = jnp.sum(s2[...], axis=0) * coef
-    for dx, dy in xy_order:
-        push(done, grad_out.at[mine], 6, part_recv.at[x], at_xy(dx, dy))
     done_copy = pltpu.make_async_copy(done, grad_out.at[mine], out_sem.at[2])
     done_copy.start()
     done_copy.wait()
     for dx in reversed(ring(nx)):
-        bx = (x + dx) % nx
+        bx = xs[dx]
         rows = pl.ds(pl.multiple_of(keep_row + bx * x_rows, x_rows), x_rows)
         count = ny - 1 if dx == 0 else ny
         drain(grad_out.at[pl.ds(0, count * piece)], part_recv.at[bx])
-        push(grad_out.at[rows], grad_out.at[rows], 7, ar_recv.at[5], partner)
-    drain(grad_out.at[pl.ds(0, half_rows)], ar_recv.at[5])
+        push(grad_out.at[rows], grad_out.at[rows], 5, ar_recv.at[3], partner)
+    drain(grad_out.at[pl.ds(0, half_rows)], ar_recv.at[3])
 
     halo_sent(win0, blocks_dev, 0)
     for turn, win in enumerate(wins):
         halo_sent(win, mesh_dev, turn + 1)
     drain(st0.at[pl.ds(0, 1)], ar_send.at[0])
     drain(grad.at[pl.ds(0, half_rows)], ar_send.at[1])
-    drain(st1.at[pl.ds(0, others)], ar_send.at[2])
-    drain(s1.at[pl.ds(0, others)], ar_send.at[3])
-    drain(st2.at[pl.ds(0, nz - 1)], ar_send.at[4])
-    drain(s2.at[pl.ds(0, nz - 1)], ar_send.at[5])
-    drain(s1.at[pl.ds(0, others)], ar_send.at[6])
-    drain(grad_out.at[pl.ds(0, half_rows)], ar_send.at[7])
+    drain(s1.at[pl.ds(0, others)], ar_send.at[2])
+    drain(s2.at[pl.ds(0, nz - 1)], ar_send.at[3])
+    drain(grad_out.at[pl.ds(0, others * piece)], ar_send.at[4])
+    drain(grad_out.at[pl.ds(0, half_rows)], ar_send.at[5])
     pred_copy.wait()
     loss_copy.wait()
 
@@ -538,6 +554,7 @@
             pltpu.VMEM((6, 2, width, width), BF16),
             pltpu.VMEM((2, width, n_var), BF16),
             pltpu.VMEM((2, points, width), BF16),
+            pltpu.VMEM((2, points, n_var), BF16),
             pltpu.VMEM((points, width), F32),
             pltpu.VMEM((2, points, lanes(5 * mesh_dev) + 4 * mesh_dev), BF16),
             pltpu.VMEM((9 * blocks_dev, width), F32),
@@ -547,27 +564,37 @@
             pltpu.VMEM((points, n_var), F32),
             pltpu.VMEM((width, n_var), F32),
             pltpu.VMEM((width // 2, n_var), F32),
-            pltpu.VMEM((width // 2, n_var), F32),
-            pltpu.VMEM((n_lon // 2 * ny, piece, n_var), F32),
-            pltpu.VMEM((nz, piece, n_var), F32),
+            pltpu.VMEM((n_lon // 2 * ny, piece + 2, n_var), F32),
+            pltpu.VMEM((n_lon // 2 * ny, piece + 2, n_var), F32),
+            pltpu.VMEM((nz, piece + 2, n_var), F32),
             pltpu.VMEM((piece, n_var), F32),
             pltpu.VMEM((1, n_var), F32),
             pltpu.VMEM((2, 2, n_var), F32),
-            pltpu.VMEM((n_lon // 2 * ny, 2, n_var), F32),
-            pltpu.VMEM((nz, 2, n_var), F32),
             pltpu.SemaphoreType.DMA((19,)),
             pltpu.SemaphoreType.DMA((3,)),
             pltpu.SemaphoreType.DMA((4, 4)),
             pltpu.SemaphoreType.DMA((4,)),
+            pltpu.SemaphoreType.DMA((1,)),
             pltpu.SemaphoreType.DMA((n_lon // 2,)),
-            pltpu.SemaphoreType.DMA((n_lon // 2,)),
+            pltpu.SemaphoreType.DMA((4,)),
             pltpu.SemaphoreType.DMA((6,)),
-            pltpu.SemaphoreType.DMA((8,)),
         ],
         compiler_params=pltpu.CompilerParams(
             collective_id=0, has_side_effects=True, vmem_limit_bytes=28 << 20
         ),
     )(*[pltpu.with_memory_space_constraint(a, pltpu.HBM) for a in operands])
+    pred, grad = pl.pallas_call(
+        place_kernel,
+        name="place",
+        out_shape=(
+            jax.ShapeDtypeStruct((points, n_var), F32),
+            jax.ShapeDtypeStruct((width, n_var), F32),
+        ),
+        in_specs=[hbm] * 2,
+        out_specs=(hbm, hbm),
+        scratch_shapes=[pltpu.SemaphoreType.DMA((2,))],
+        compiler_params=pltpu.CompilerParams(vmem_limit_bytes=1 << 20),
+    )(pred, grad)
     return (pred, loss[0, 0], grad)
 
 

time: 71.1 us -> 69.4 us (0.976)
  local copies, waits for them, and re-layouts: 1.36 us -> 0 us
    unnamed x2 -> x0, local copies, waits for them, and re-layouts: 1.36 us -> none
    pallas_call x1, Pallas kernels: 67.8 us -> 66.7 us  [shards(): pl.pallas_call(functools.partial(program_kernel, n_lat, n_lon, nz), name=...]
    pallas_call x0 -> x1, Pallas kernels: none -> 0.76 us  [shards(): pl.pallas_call(place_kernel, name='place', out_shape=(jax.ShapeDtypeStruc...]
where the time goes in v4:
time: 69.4 us; the launch traced here: 69.3 us
  Pallas kernels  67.5 us (97%)
  between operations  1.81 us (3%)
    pallas_call x1, Pallas kernels, shards(): pl.pallas_call(functools.partial(program_kernel, n_lat, n_lon, nz), name=...  66.7 us

profile of v4, /device:TPU:1, one launch (start us, length us, event | category | flops | bytes accessed | tf_op | source)
XLA Modules:
  0.0 69.3 jit_solution(16987753992948191929)
XLA Ops:
  0.6 66.7 %forecast_step.1 = (f32[256,128]{1,0:T(8,128)S(1)}, f32[1,128]{1,0:T(1,128)S(1)}, f32[512,128]{1,0:T(8,128)S(1)}) custom-call(f32[256,512]{1,0:T(8,128)} %grid_hbm.1, f32[256,128]{1,0:T(8,128)} %target_hbm.1, f32[512,512]{1,0:T(8,128)} %w_enc_hbm.1, f32[2,512,512]{2,1,0:T(8,128)} %w_self_hbm.1, f32[2,512,512]{2,1,0:T(8,128)} %w_nbr_hbm.1, ...), custom_call_target="tpu_custom_call" | custom-call | tf_op jit(solution)/shard_map/forecast_step/pallas_call | solution.py:535
  67.3 0.8 %place.1 = (f32[256,128]{1,0:T(8,128)}, f32[512,128]{1,0:T(8,128)}) custom-call(f32[256,128]{1,0:T(8,128)S(1)} %get-tuple-element.8.pred_in, f32[512,128]{1,0:T(8,128)S(1)} %get-tuple-element.9.grad_in), custom_call_target="tpu_custom_call" | custom-call | tf_op jit(solution)/shard_map/place/pallas_call | solution.py:586

commit v5 on v4

--- a/solution.py
+++ b/solution.py
@@ -356,12 +356,12 @@
         nrm = center / jnp.sqrt(spread + EPS)
         self_part = mm3(split(nrm), weight(2 + 2 * layer))
         if layer == 0:
+            halo_forward(win, mesh_dev, layer + 1)
             for ready, which in ((6, 4), (7, 5)):
                 later[ready].wait()
                 split_weight(which)
             later[3].wait()
             split_weight(1)
-            halo_forward(win, mesh_dev, layer + 1)
             later[1].wait()
             later[2].wait()
             factors = m_w[...].T

time: 69.4 us -> 69.6 us (level)
  no operation moved by 1% of the time
where the time goes in v5:
time: 69.6 us; the launch traced here: 69.4 us
  Pallas kernels  67.6 us (97%)
  between operations  1.81 us (3%)
    pallas_call x1, Pallas kernels, shards(): pl.pallas_call(functools.partial(program_kernel, n_lat, n_lon, nz), name=...  66.9 us

profile of v5, /device:TPU:1, one launch (start us, length us, event | category | flops | bytes accessed | tf_op | source)
XLA Modules:
  0.0 69.4 jit_solution(12881644927164914296)
XLA Ops:
  0.6 66.9 %forecast_step.1 = (f32[256,128]{1,0:T(8,128)S(1)}, f32[1,128]{1,0:T(1,128)S(1)}, f32[512,128]{1,0:T(8,128)S(1)}) custom-call(f32[256,512]{1,0:T(8,128)} %grid_hbm.1, f32[256,128]{1,0:T(8,128)} %target_hbm.1, f32[512,512]{1,0:T(8,128)} %w_enc_hbm.1, f32[2,512,512]{2,1,0:T(8,128)} %w_self_hbm.1, f32[2,512,512]{2,1,0:T(8,128)} %w_nbr_hbm.1, ...), custom_call_target="tpu_custom_call" | custom-call | tf_op jit(solution)/shard_map/forecast_step/pallas_call | solution.py:535
  67.5 0.8 %place.1 = (f32[256,128]{1,0:T(8,128)}, f32[512,128]{1,0:T(8,128)}) custom-call(f32[256,128]{1,0:T(8,128)S(1)} %get-tuple-element.8.pred_in, f32[512,128]{1,0:T(8,128)S(1)} %get-tuple-element.9.grad_in), custom_call_target="tpu_custom_call" | custom-call | tf_op jit(solution)/shard_map/place/pallas_call | solution.py:586
